TPU v7x, 32 devices: a whole 2x2x4 slice. The times are simulated.
32 devices in a mesh: frame: 16 (over z, y, x), row: 2 (over core).
Axes of the slice: x: 2, y: 2, z: 4, core: 2. Of those that a mesh axis runs over, the one named last changes fastest.
Arguments:
- tokens: bfloat16 [16, 2, 128, 2048], P('frame', 'row'), may hold values from -6 to 6
- cotangent: bfloat16 [16, 2, 128, 2048], P('frame', 'row'), may hold values from -6 to 6
- timestep: int32 [1], replicated, may hold values from 0 to 999
- mod_weight: bfloat16 [256, 4096], P(None, 'frame'), may hold values from -0.375 to 0.375
- proj_weight: bfloat16 [2048, 256], P('frame'), may hold values from -0.125 to 0.125
- step_weight: bfloat16 [2048, 32], P('frame'), may hold values from -0.125 to 0.125
- step_bias: float32 [32], replicated, may hold values from -1 to 1
- rate_space: float32 [32], replicated, may hold values from 0.001171875 to 0.05
- rate_time: float32 [32], replicated, may hold values from 0.01875 to 1
- skip_gain: float32 [32], replicated, may hold values from 0.5 to 1.5
Outputs:
- mixed: bfloat16 [16, 2, 128, 2048], P('frame', 'row')
- d_tokens: bfloat16 [16, 2, 128, 2048], P('frame', 'row')
- grad_proj: float32 [2048, 256], P('frame')
- grad_step: float32 [2048, 32], P('frame')
- grad_mod: float32 [256, 4096], P(None, 'frame')
All inputs are finite; a program needn't handle non-finite values.
Results may differ from a plain program's by a relative error of at most 0.015.
Values may be sent and summed in bfloat16 or wider, within the bound.
No kernel may reach another device: no remote copies, remote signals or barrier semaphores. Data moves between devices by JAX's collectives and lax.ppermute only.
A program may use at most 64 MiB of HBM per device.

v0:
```python
import functools
import math

import jax
import jax.numpy as jnp
from jax import lax
from jax.experimental import pallas as pl
from jax.experimental.pallas import tpu as pltpu
from jax.sharding import PartitionSpec as P


norm_eps = 1e-05
LANES = 128
LOG2E = math.log2(math.e)
f32 = jnp.float32
bf16 = jnp.bfloat16
EXACT = lax.Precision.HIGHEST


def time_embed(timestep, embed_dim):
    half_dim = embed_dim // 2
    place = (jnp.arange(embed_dim) % half_dim).astype(f32)
    frequency = jnp.exp(-math.log(10000.0) * place / half_dim)
    angles = timestep.astype(f32)[:, None] * frequency[None, :]
    lower = jnp.arange(embed_dim)[None, :] < half_dim
    return jax.nn.silu(jnp.where(lower, jnp.cos(angles), jnp.sin(angles)))


def to_tiles(a):
    f, r, c = a.shape
    if r % 8 == 0 and c % LANES == 0:
        a = a.reshape(f, r // 8, 8, c // LANES, LANES).transpose(0, 1, 3, 2, 4)
    return a.reshape(f, r * c // LANES, LANES)


def from_tiles(a, r, c):
    f = a.shape[0]
    if r % 8 == 0 and c % LANES == 0:
        a = a.reshape(f, r // 8, c // LANES, 8, LANES).transpose(0, 1, 3, 2, 4)
    return a.reshape(f, r, c)


def exchange(packed):
    return lax.all_to_all(packed, "frame", split_axis=0, concat_axis=0, tiled=True)


def mm(a, b, ca, cb):
    return lax.dot_general(a, b, (((ca,), (cb,)), ((), ())), preferred_element_type=f32)


def exact(a, b, ca, cb):
    return lax.dot_general(
        a, b, (((ca,), (cb,)), ((), ())), preferred_element_type=f32, precision=EXACT
    )


def split(a):
    high = a.astype(bf16)
    return high, (a - high.astype(f32)).astype(bf16)


def head_map(heads, width):
    size = width // heads
    own = lax.broadcasted_iota(jnp.int32, (heads, width), 0)
    lane = lax.broadcasted_iota(jnp.int32, (heads, width), 1)
    return jnp.where(lane // size == own, 1.0, 0.0).astype(bf16)


def sequence_mask(length, sites):
    later = lax.broadcasted_iota(jnp.int32, (length, length), 0)
    earlier = lax.broadcasted_iota(jnp.int32, (length, length), 1)
    keep = later >= earlier
    if sites > 1:
        keep = keep & (later % sites == earlier % sites)
    return jnp.where(keep, 1.0, 0.0).astype(f32)


def blocks(width):
    return [(j, slice(j * LANES, (j + 1) * LANES)) for j in range(width // LANES)]


def spread_rows(rows, length):
    count = rows.shape[0]
    if count == 1:
        return rows
    part = (length // count, rows.shape[1])
    return jnp.concatenate([jnp.broadcast_to(rows[c : c + 1], part) for c in range(count)], axis=0)


def normalize_into(tok_ref, shift_ref, gain_ref, x_ref, read=None):
    length, width = tok_ref.shape
    total = jnp.zeros((length, LANES), f32)
    for _, sl in blocks(width):
        if read is None:
            v = tok_ref[:, sl].astype(f32)
        else:
            v = read(sl)
            tok_ref[:, sl] = v.astype(bf16)
        total = total + v * v
    mean = jnp.sum(total, axis=1, keepdims=True) / width
    inverse = lax.rsqrt(mean + norm_eps)
    for _, sl in blocks(width):
        unit = tok_ref[:, sl].astype(f32) * inverse
        gain = spread_rows(gain_ref[:, sl], length)
        shift = spread_rows(shift_ref[:, sl], length)
        x_ref[:, sl] = (unit * (1.0 + gain) + shift).astype(bf16)
    return inverse


def steps_of(logits, bias, rate, mask):
    z = logits.astype(f32) + bias
    step = jnp.maximum(z, 0.0) + jnp.log1p(jnp.exp(-jnp.abs(z)))
    log_decay = -step * rate
    parts, mask = thirds_of(log_decay), tripled(mask, 1)
    cum = mm(mask, parts, 1, 0)
    return z, step, cum, (cum * LOG2E, mm(parts, mask, 0, 1) * LOG2E)


def thirds_of(a):
    high, rest = split(a)
    high_rest = a - high.astype(f32)
    return jnp.concatenate([high, rest, (high_rest - rest.astype(f32)).astype(bf16)], axis=0)


def tripled(mask, axis):
    return jnp.concatenate([mask.astype(bf16)] * 3, axis=axis)


def halves_of(a):
    return jnp.concatenate(split(a), axis=1)


def doubled(lanes_of):
    return jnp.concatenate([lanes_of, lanes_of], axis=0)


def scan_block(j, x, grad, step_wide, scores, cums, heads, width, d_scores):
    size = width // heads
    per_block = LANES // size
    length = x.shape[0]
    stepped = (x.astype(f32) * step_wide).astype(bf16)
    lane = lax.broadcasted_iota(jnp.int32, x.shape, 1)
    inside = [lane // size == i for i in range(per_block)]
    zero = jnp.zeros_like(x)
    steppeds = jnp.concatenate([jnp.where(own, stepped, zero) for own in inside], axis=0)
    grads = jnp.concatenate([jnp.where(own, grad, zero) for own in inside], axis=0)
    d_weights = mm(grads, stepped, 1, 1)
    weights = []
    for i in range(per_block):
        h = j * per_block + i
        decay = jnp.exp2(jnp.minimum(cums[0][:, h : h + 1] - cums[1][h : h + 1, :], 0.0))
        d_scores = d_scores + d_weights[i * length : (i + 1) * length] * decay
        weights.append((scores * decay).astype(bf16))
    out = mm(jnp.concatenate(weights, axis=1), steppeds, 1, 0)
    d_stepped = mm(jnp.concatenate(weights, axis=0), grads, 0, 0)
    return stepped, out, d_stepped, d_scores


def put(sums_ref, which, sl, value):
    length = value.shape[0]
    sums_ref[which * length : (which + 1) * length, sl] = value.astype(bf16)


def head_sums(sums_ref, lanes_of, length):
    sums = mm(sums_ref[...], lanes_of, 1, 1)
    return [sums[at : at + length] for at in range(0, sums.shape[0], length)]


def wide_blocks(width):
    return [(slice(at, at + 2 * LANES)) for at in range(0, width, 2 * LANES)]


def start_kernel(ids_ref, tok_ref, grad_ref, proj_hbm, step_hbm, mod_hbm, active_ref, sent_ref, pay_ref,
                 proj_ref, step_ref, mod_ref, sems):
    pairs = [(proj_hbm, proj_ref), (step_hbm, step_ref), (mod_hbm, mod_ref)]
    pairs += [(tok_ref, sent_ref.at[:, 0]), (grad_ref, sent_ref.at[:, 1])]
    copies = [
        pltpu.make_async_copy(src, dst, sems.at[n]) for n, (src, dst) in enumerate(pairs)
    ]
    for copy in copies:
        copy.start()
    row = ids_ref[1]
    part, pair = proj_ref.shape[0] // 2, proj_ref.shape[1]
    copies[0].wait()
    own = proj_ref[pl.ds(pl.multiple_of(row * part, part), part), :]
    at = 0
    for _, sl in blocks(pair):
        pay_ref[at : at + part, :] = own[:, sl]
        at += part
    copies[1].wait()
    part = step_ref.shape[0] // 2
    pay_ref[at : at + part, :] = step_ref[pl.ds(pl.multiple_of(row * part, part), part), :]
    at += part
    copies[2].wait()
    own = mm(active_ref[...], mod_ref[...], 1, 0)
    high = own.astype(bf16).astype(f32)
    pieces = [piece[:, sl] for piece in (high, own - high) for _, sl in blocks(own.shape[1])]
    pieces.append(jnp.zeros((8 - len(pieces), LANES), f32))
    pay_ref[at : at + 8, :] = jnp.concatenate(pieces, axis=0).astype(bf16)
    copies[3].wait()
    copies[4].wait()


def unpack_kernel(radix, ids_ref, *refs):
    own_refs, other_refs = refs[:radix], refs[radix : 2 * radix]
    proj_ref, step_ref, shift_ref, gain_ref = refs[2 * radix :]
    me, row = ids_ref[0], ids_ref[1]
    width, pair = proj_ref.shape
    frames = radix * radix
    depth = width // frames
    part, heads = depth // 2, step_ref.shape[0] // 2
    cols = 2 * width // frames
    for i in range(frames):
        source = jnp.bitwise_xor(me, (i % radix) * radix + i // radix)
        near, far = i // radix, i % radix
        for ref, half in ((own_refs[near], row), (other_refs[near], 1 - row)):
            rows = pl.ds(pl.multiple_of(source * depth + half * part, part), part)
            at = 0
            for _, sl in blocks(pair):
                proj_ref[rows, sl] = ref[far, at : at + part, :]
                at += part
            rows = pl.ds(pl.multiple_of(half * heads, heads), heads)
            lanes = pl.ds(pl.multiple_of(source * depth, depth), depth)
            step_ref[rows, lanes] = ref[far, at : at + heads, :]
            at += heads
        own = own_refs[near][far, at : at + 8, :].astype(f32)
        count = cols // LANES
        lanes_at = jnp.bitwise_and(source, frames // 2 - 1) * cols
        for k in range(count):
            value = own[k : k + 1, :] + own[count + k : count + k + 1, :]
            lanes = pl.ds(pl.multiple_of(lanes_at + k * LANES, LANES), LANES)

            @pl.when(source < frames // 2)
            def _():
                shift_ref[:, lanes] = value

            @pl.when(source >= frames // 2)
            def _():
                gain_ref[:, lanes] = value


def finish_mod_kernel(factor, at, sums_ref, active_ref, mod_ref):
    rest = jnp.zeros((7, active_ref.shape[1]), f32)
    active = jnp.concatenate([active_ref[...].astype(f32), rest], axis=0)
    for k, sl in blocks(mod_ref.shape[1]):
        own = jnp.broadcast_to(sums_ref[at + k : at + k + 1, :] * factor, (8, LANES))
        mod_ref[:, sl] = exact(active, own, 0, 0)


def finish_kernel(factor, ids_ref, own_ref, other_ref, proj_ref, step_ref):
    row = ids_ref[1]
    pair = proj_ref.shape[1]
    part, heads = proj_ref.shape[0] // 2, step_ref.shape[0] // 2
    for ref, half in ((own_ref, row), (other_ref, 1 - row)):
        rows = pl.ds(pl.multiple_of(half * part, part), part)
        at = 0
        for _, sl in blocks(pair):
            proj_ref[rows, sl] = ref[at : at + part, :] * factor
            at += part
        step_ref[pl.ds(pl.multiple_of(half * heads, heads), heads), :] = ref[at : at + heads, :] * factor


def site_fast_kernel(sites, got_ref, *refs):
    inputs, (small_ref, sent_hbm, x_hbm, gmod_hbm, dc_ref, dl_ref) = refs[:4], refs[4:10]
    inputs = (*inputs, small_ref[0:1, :], small_ref[1:2, :])
    tok_ref, sent_ref, x_ref, gmod_ref, sems = refs[10:15]
    scratch = refs[15:]
    frames, width = got_ref.shape[0], got_ref.shape[3]

    def read(which):
        return lambda sl: got_ref[:, which, :, sl].astype(f32).reshape(frames * sites, LANES)

    class Grad:
        def __getitem__(self, at):
            return read(1)(at[1]).astype(bf16)

    parts = 8
    share = width // parts
    copies = []

    def begin(source, target):
        copy = pltpu.make_async_copy(source, target, sems.at[len(copies)])
        copy.start()
        copies.append(copy)

    def send(which, p):
        at = (slice(None), which, slice(None), slice(p * share, (p + 1) * share))
        begin(sent_ref.at[at], sent_hbm.at[at])

    class Packed:
        def __init__(self, which):
            self.which = which

        def __setitem__(self, at, value):
            if not copies:
                begin(x_ref, x_hbm)
            value = value.astype(f32).reshape(frames, sites, value.shape[1])
            sent_ref[:, self.which, :, at[1]] = value.astype(bf16)
            if at[1].stop % share == 0:
                send(self.which, at[1].stop // share - 1)

    site_kernel(
        sites,
        tok_ref,
        Grad(),
        *inputs,
        Packed(0),
        Packed(1),
        dc_ref,
        dl_ref,
        gmod_ref,
        x_ref,
        *scratch,
        read=read(0),
    )
    begin(gmod_ref, gmod_hbm)
    for copy in copies:
        copy.wait()


def site_kernel(
    sites,
    tok_ref,
    grad_ref,
    shift_ref,
    gain_ref,
    proj_ref,
    step_ref,
    bias_ref,
    rate_ref,
    out_ref,
    back_ref,
    gproj_ref,
    gstep_ref,
    gmod_ref,
    x_ref,
    dn_ref,
    sums_ref,
    read=None,
):
    length, width = tok_ref.shape
    heads = step_ref.shape[0]
    state = proj_ref.shape[1] // 2
    clips = shift_ref.shape[0]
    inverse = normalize_into(tok_ref, shift_ref, gain_ref, x_ref, read)
    lanes_of = head_map(heads, width)
    mask = sequence_mask(length, sites)
    coeffs = mm(x_ref[...], proj_ref[...], 1, 0).astype(bf16)
    logits = mm(x_ref[...], step_ref[...], 1, 1).astype(bf16)
    rate = rate_ref[...]
    z, step, _, cums = steps_of(logits, bias_ref[...], rate, mask)
    b_part, c_part = coeffs[:, :state], coeffs[:, state:]
    scores = mm(c_part, b_part, 1, 1) * (mask / state)
    step_parts, twice = halves_of(step), doubled(lanes_of)
    d_scores = jnp.zeros((length, length), f32)
    for j, sl in blocks(width):
        x, grad = x_ref[:, sl], grad_ref[:, sl]
        step_wide = mm(step_parts, twice[:, sl], 1, 0)
        stepped, out, d_stepped, d_scores = scan_block(
            j, x, grad, step_wide, scores, cums, heads, width, d_scores
        )
        out_ref[:, sl] = out.astype(bf16)
        dn_ref[:, sl] = (step_wide * d_stepped).astype(bf16)
        put(sums_ref, 0, sl, grad.astype(f32) * out - stepped.astype(f32) * d_stepped)
        put(sums_ref, 1, sl, x.astype(f32) * d_stepped)
    d_cum, d_step = head_sums(sums_ref, lanes_of, length)
    d_log = mm(tripled(mask, 0), thirds_of(d_cum), 0, 0)
    d_logits = (jax.nn.sigmoid(z) * (d_step - rate * d_log)).astype(bf16)
    d_scores = (d_scores * (mask / state)).astype(bf16)
    d_coeffs = jnp.concatenate(
        [mm(d_scores, c_part, 0, 0), mm(d_scores, b_part, 1, 0)], axis=1
    ).astype(bf16)
    clip = lax.broadcasted_iota(jnp.int32, (8, length), 1) // (length // clips)
    clip_row = lax.broadcasted_iota(jnp.int32, (8, length), 0)
    pick = jnp.where(clip == clip_row, 1.0, 0.0).astype(bf16)
    for sl in wide_blocks(width):
        back = (
            dn_ref[:, sl].astype(f32)
            + mm(d_coeffs, proj_ref[sl, :], 1, 1)
            + mm(d_logits, step_ref[:, sl], 1, 0)
        )
        low = back.astype(bf16)
        back_ref[:, sl] = low
        scaled = (back * (tok_ref[:, sl].astype(f32) * inverse)).astype(bf16)
        gmod_ref[0:clips, sl] = mm(pick, low, 1, 0)[0:clips]
        gmod_ref[clips : 2 * clips, sl] = mm(pick, scaled, 1, 0)[0:clips]
        if gproj_ref.shape == (width, 2 * state):
            gproj_ref[sl, :] = mm(x_ref[:, sl], d_coeffs, 0, 0)
            gstep_ref[:, sl] = mm(d_logits, x_ref[:, sl], 0, 0)
    if gproj_ref.shape != (width, 2 * state):
        gproj_ref[...] = d_coeffs
        gstep_ref[...] = d_logits


def band_fast_kernel(ids_ref, *refs):
    small_ref, give_ref = refs[6], refs[-1]
    inputs = (*refs[:6], small_ref[0:1, :], small_ref[2:3, :])
    band_kernel(*inputs, *refs[7:-1], None, None, give_ref, first=ids_ref[1] == 0)


def band_kernel(
    tok_ref,
    grad_ref,
    shift_ref,
    gain_ref,
    proj_ref,
    step_ref,
    bias_ref,
    rate_ref,
    x_ref,
    coeffs_ref,
    logits_ref,
    inverse_ref,
    decay_ref,
    end_ref,
    own_ref,
    first=None,
):
    length, width = tok_ref.shape
    heads = step_ref.shape[0]
    state = proj_ref.shape[1] // 2
    inverse_ref[...] = normalize_into(tok_ref, shift_ref, gain_ref, x_ref)
    twice = doubled(head_map(heads, width))
    mask = sequence_mask(length, 1)
    coeffs = mm(x_ref[...], proj_ref[...], 1, 0).astype(bf16)
    logits = mm(x_ref[...], step_ref[...], 1, 1).astype(bf16)
    coeffs_ref[...] = coeffs
    logits_ref[...] = logits
    _, step, cum, _ = steps_of(logits, bias_ref[...], rate_ref[...], mask)
    last = cum[length - 1 : length, :]
    b_part, c_part = coeffs[:, :state], coeffs[:, state:]
    if first is not None:
        gain = halves_of(jnp.where(first, jnp.exp(last - cum) * step, jnp.exp(cum) / state))
        other = jnp.where(first, b_part, c_part)
        for _, sl in blocks(width):
            value = jnp.where(first, x_ref[:, sl], grad_ref[:, sl]).astype(f32)
            value = (value * mm(gain, twice[:, sl], 1, 0)).astype(bf16)
            own_ref[sl, :] = mm(value, other, 0, 0).astype(bf16)
        return
    decay_ref[...] = jnp.exp(last)
    lead = halves_of(jnp.exp(last - cum) * step)
    reach = halves_of(jnp.exp(cum) / state)
    for _, sl in blocks(width):
        lead_wide = mm(lead, twice[:, sl], 1, 0)
        reach_wide = mm(reach, twice[:, sl], 1, 0)
        scaled = (x_ref[:, sl].astype(f32) * lead_wide).astype(bf16)
        faded = (grad_ref[:, sl].astype(f32) * reach_wide).astype(bf16)
        end_ref[sl, :] = mm(scaled, b_part, 0, 0).astype(bf16)
        own_ref[sl, :] = mm(faded, c_part, 0, 0).astype(bf16)


def terms_kernel(radix, ids_ref, x_ref, dc_ref, dl_ref, gmod_ref, site_x, site_dc, site_dl, site_gmod, *refs):
    me, first = ids_ref[0], ids_ref[1] == 0
    width = x_ref.shape[1]
    coeffs = jnp.concatenate([dc_ref[...], site_dc[...]], axis=0)
    logits = jnp.concatenate([dl_ref[...], site_dl[...]], axis=0)
    share = 2 * width // LANES // (radix * radix)
    half = radix * radix // 2

    def put_halves(keep_ref, give_ref, e, at, value):
        part = value.shape[0] // 2
        own = jnp.where(first, value[:part], value[part:]).astype(bf16)
        other = jnp.where(first, value[part:], value[:part]).astype(bf16)
        for _, sl in blocks(value.shape[1]):
            keep_ref[e, at : at + part, :] = own[:, sl]
            give_ref[e, at : at + part, :] = other[:, sl]
            at += part
        return at

    for d in (*range(1, radix), 0):
        keep_ref, give_ref = refs[d], refs[radix + d]
        for e in range(radix):
            frame = jnp.bitwise_xor(me, e * radix + d)
            sl = pl.ds(pl.multiple_of(frame * LANES, LANES), LANES)
            tall = jnp.concatenate([x_ref[:, sl], site_x[:, sl]], axis=0)
            at = put_halves(keep_ref, give_ref, e, 0, mm(tall, coeffs, 0, 0))
            at = put_halves(keep_ref, give_ref, e, at, mm(logits, tall, 0, 0))
            start = jnp.bitwise_and(frame, half - 1) * share * LANES
            rows = []
            for k in range(share):
                lanes = pl.ds(pl.multiple_of(start + k * LANES, LANES), LANES)
                both = gmod_ref[:, lanes] + site_gmod[:, lanes]
                rows.append(jnp.where(frame < half, both[0:1], both[1:2]))
            rows.append(jnp.zeros((8 - len(rows), LANES), f32))
            rows = jnp.concatenate(rows, axis=0).astype(bf16)
            keep_ref[e, at : at + 8, :] = rows
            give_ref[e, at : at + 8, :] = rows


def space_fast_kernel(ids_ref, arrived_ref, *refs):
    inputs, small_ref, outs = refs[:8], refs[8], refs[9:]
    inputs = (*inputs, *(small_ref[n : n + 1, :] for n in (0, 2, 3)))
    space_kernel(*inputs, arrived_ref, None, None, None, *outs, first=ids_ref[1] == 0)


def space_kernel(
    tok_ref,
    grad_ref,
    x_ref,
    coeffs_ref,
    logits_ref,
    inverse_ref,
    proj_ref,
    step_ref,
    bias_ref,
    rate_ref,
    skip_ref,
    state_ref,
    later_ref,
    gproj_in,
    gstep_in,
    mix_ref,
    pre_ref,
    gproj_ref,
    gstep_ref,
    gmod_ref,
    dn_ref,
    sums_ref,
    first=None,
):
    length, width = tok_ref.shape
    heads = step_ref.shape[0]
    state = proj_ref.shape[1] // 2
    lanes_of = head_map(heads, width)
    twice = doubled(lanes_of)
    mask = sequence_mask(length, 1)
    coeffs = coeffs_ref[...]
    rate = rate_ref[...]
    z, step, cum, cums = steps_of(logits_ref[...], bias_ref[...], rate, mask)
    last = cum[length - 1 : length, :]
    rest = jnp.exp(last - cum)
    lead, reach = rest * step, jnp.exp(cum) / state
    b_part, c_part = coeffs[:, :state], coeffs[:, state:]
    scores = mm(c_part, b_part, 1, 1) * (mask / state)
    skip = jnp.broadcast_to(skip_ref[...], (8, heads))
    if first is None:
        parts = [step, lead, reach, skip]
    else:
        parts = [step, jnp.where(first, lead, reach), skip]
        chosen = jnp.where(first, b_part, c_part)
        is_first = jnp.where(first, 1.0, 0.0).astype(f32)
        is_second = 1.0 - is_first
    parts = jnp.concatenate([halves_of(part) for part in parts], axis=0)
    d_scores = jnp.zeros((length, length), f32)
    d_b = jnp.zeros((length, state), f32)
    d_c = jnp.zeros((length, state), f32)
    d_end = jnp.zeros((heads, state), f32)
    for j, sl in blocks(width):
        x, grad = x_ref[:, sl], grad_ref[:, sl]
        wide_parts = mm(parts, twice[:, sl], 1, 0)
        step_wide, lead_wide = wide_parts[:length], wide_parts[length : 2 * length]
        skip = wide_parts[-8:-7]
        stepped, out, d_stepped, d_scores = scan_block(
            j, x, grad, step_wide, scores, cums, heads, width, d_scores
        )
        if first is None:
            x, wide = x.astype(f32), grad.astype(f32)
            reach_wide = wide_parts[2 * length : 3 * length]
            before, later = state_ref[sl, :], later_ref[sl, :]
            total = out + mm(c_part, before, 1, 1) * reach_wide
            d_c = d_c + mm((wide * reach_wide).astype(bf16), before, 1, 0)
            d_b = d_b + mm((x * lead_wide).astype(bf16), later, 1, 0)
            d_scaled = mm(b_part, later, 1, 1)
            d_x = step_wide * d_stepped + d_scaled * lead_wide
            both = split(before.astype(f32) * later.astype(f32))
            d_end = d_end + mm(lanes_of[:, sl], both[0], 1, 0) + mm(lanes_of[:, sl], both[1], 1, 0)
        else:
            arrived = state_ref[sl, :]
            value = jnp.where(first, x, grad).astype(f32)
            d_b = d_b + mm((value * lead_wide).astype(bf16), arrived, 1, 0)
            x, wide = x.astype(f32), grad.astype(f32)
            d_scaled = mm(chosen, arrived, 1, 1)
            carried = d_scaled * lead_wide
            total = out + carried * is_second
            d_x = step_wide * d_stepped + carried * is_first
            d_scaled = d_scaled * is_first
        mix_ref[:, sl] = total + skip * x
        dn_ref[:, sl] = d_x.astype(bf16) + (wide * skip).astype(bf16)
        put(sums_ref, 0, sl, wide * total - stepped.astype(f32) * d_stepped)
        put(sums_ref, 1, sl, x * d_stepped)
        put(sums_ref, 2, sl, x * d_scaled)
    d_cum, d_step, d_lead = head_sums(sums_ref, lanes_of, length)
    d_step = d_step + d_lead * rest
    fall = d_lead * lead
    d_cum = d_cum - fall
    end_sum = jnp.sum(fall, axis=0, keepdims=True)
    if first is None:
        ones = jnp.ones((8, state), f32)
        end_sum = end_sum + exact(ones, d_end, 1, 1)[0:1, :] * jnp.exp(last)
    else:
        d_b, d_c = d_b * is_first, d_b * is_second
    d_log = mm(tripled(mask, 0), thirds_of(d_cum), 0, 0) + end_sum
    d_logits = (jax.nn.sigmoid(z) * (d_step - rate * d_log)).astype(bf16)
    d_scores = (d_scores * (mask / state)).astype(bf16)
    d_coeffs = jnp.concatenate(
        [mm(d_scores, c_part, 0, 0) + d_b, mm(d_scores, b_part, 1, 0) + d_c], axis=1
    ).astype(bf16)
    inverse = inverse_ref[...]
    if gproj_in is None:
        gproj_ref[...] = d_coeffs
        gstep_ref[...] = d_logits
    for sl in wide_blocks(width):
        pre = (
            dn_ref[:, sl].astype(f32)
            + mm(d_coeffs, proj_ref[sl, :], 1, 1)
            + mm(d_logits, step_ref[:, sl], 1, 0)
        )
        pre_ref[:, sl] = pre
        scaled = pre * (tok_ref[:, sl].astype(f32) * inverse)
        gmod_ref[0:1, sl] = jnp.sum(pre, axis=0, keepdims=True)
        gmod_ref[1:2, sl] = jnp.sum(scaled, axis=0, keepdims=True)
        if gproj_in is not None:
            gproj_ref[sl, :] = (gproj_in[sl, :] + mm(x_ref[:, sl], d_coeffs, 0, 0)).astype(bf16)
            gstep_ref[:, sl] = (gstep_in[:, sl] + mm(d_logits, x_ref[:, sl], 0, 0)).astype(bf16)


def last_kernel(tok_ref, inverse_ref, gain_ref, mix_ref, pre_ref, time_ref, back_ref, out_ref, dtok_ref):
    length, width = tok_ref.shape
    inverse = inverse_ref[...]
    total = jnp.zeros((length, LANES), f32)
    for _, sl in blocks(width):
        out_ref[:, sl] = (mix_ref[:, sl] + time_ref[:, sl].astype(f32)).astype(bf16)
        grad = (pre_ref[:, sl] + back_ref[:, sl].astype(f32)) * (1.0 + gain_ref[:, sl])
        total = total + grad * tok_ref[:, sl].astype(f32)
    inner = jnp.sum(total, axis=1, keepdims=True) / width
    inner = inner * inverse * inverse * inverse
    for _, sl in blocks(width):
        grad = (pre_ref[:, sl] + back_ref[:, sl].astype(f32)) * (1.0 + gain_ref[:, sl])
        dtok_ref[:, sl] = (grad * inverse - tok_ref[:, sl].astype(f32) * inner).astype(bf16)


def last_fast_kernel(tok_ref, inverse_ref, gain_ref, mix_ref, pre_ref, came_ref, *outs):
    class Packed:
        def __init__(self, which):
            self.which = which

        def __getitem__(self, at):
            value = came_ref[:, self.which, :, at[1]].astype(f32)
            return value.reshape(value.shape[0] * value.shape[1], LANES)

    last_kernel(tok_ref, inverse_ref, gain_ref, mix_ref, pre_ref, Packed(0), Packed(1), *outs)


def in_hbm(array):
    return pltpu.with_memory_space_constraint(array, pltpu.MemorySpace.HBM)


def call(kernel, outs, scratch=(), specs=None, hbm_outs=()):
    shapes = [
        pltpu.MemorySpace.HBM(s, d) if n in hbm_outs else jax.ShapeDtypeStruct(s, d)
        for n, (s, d) in enumerate(outs)
    ]
    where = {"s": pltpu.SMEM, "v": pltpu.VMEM, "h": pltpu.MemorySpace.HBM}
    spaces = {}
    if specs:
        spaces["in_specs"] = [pl.BlockSpec(memory_space=where[c]) for c in specs]
        spaces["out_specs"] = [
            pl.BlockSpec(memory_space=where["h" if n in hbm_outs else "v"]) for n in range(len(outs))
        ]
    return pl.pallas_call(
        kernel,
        out_shape=shapes,
        **spaces,
        scratch_shapes=[pltpu.VMEM(*s) if isinstance(s, tuple) else s for s in scratch],
        compiler_params=pltpu.CompilerParams(vmem_limit_bytes=24 << 20),
    )


def rows_in_order(part):
    if lax.axis_size("row") != 2:
        return lax.all_gather(part, "row")
    other = lax.ppermute(part, "row", [(0, 1), (1, 0)])
    first = lax.axis_index("row") == 0
    return jnp.stack([jnp.where(first, part, other), jnp.where(first, other, part)])


def rows_sum(part):
    if lax.axis_size("row") != 2:
        return lax.psum(part, "row")
    return part + lax.ppermute(part, "row", [(0, 1), (1, 0)])


def chain(own, decay, forward):
    count = lax.axis_size("row")
    hops = [(i, i + 1) if forward else (i + 1, i) for i in range(count - 1)]
    if count == 1:
        return jnp.zeros_like(own)
    arrived = lax.ppermute(own, "row", hops)
    wide = jnp.repeat(decay[0], own.shape[0] // decay.shape[1])[:, None]
    for _ in range(count - 2):
        passed = wide * arrived.astype(f32) + own.astype(f32)
        arrived = lax.ppermute(passed.astype(bf16), "row", hops)
    return arrived


def per_device(
    tokens,
    cotangent,
    timestep,
    mod_weight,
    proj_weight,
    step_weight,
    step_bias,
    rate_space,
    rate_time,
    skip_gain,
):
    frames = lax.axis_size("frame")
    rows = lax.axis_size("row")
    frame_id = lax.axis_index("frame")
    row_id = lax.axis_index("row")
    width = tokens.shape[-1]
    length = tokens.shape[1] * tokens.shape[2]
    clips = timestep.shape[0]
    clip_id = frame_id // (frames // clips)
    sites = length // frames
    heads = rate_space.shape[0]
    depth, pair = proj_weight.shape
    state = pair // 2
    mod_cols = mod_weight.shape[1]
    factor = (frames * rows * length) ** (-0.5)
    tok = tokens.reshape(length, width)
    grad = cotangent.reshape(length, width)

    activated = time_embed(timestep, mod_weight.shape[0]).astype(bf16)
    own_mod = jnp.dot(activated, mod_weight, preferred_element_type=f32)
    high = lax.reduce_precision(own_mod, 8, 7)
    own_mod = jnp.stack([high, own_mod - high]).astype(bf16)

    part = depth // rows
    own_proj = lax.dynamic_slice_in_dim(proj_weight, row_id * part, part, 0)
    to_all = [
        to_tiles(own_proj[None]),
        to_tiles(step_weight.T[None]),
        own_mod.reshape(1, -1, LANES),
    ]
    to_all = jnp.concatenate(to_all, axis=1)
    to_all = jnp.pad(to_all, ((0, 0), (0, -to_all.shape[1] % 8), (0, 0)))
    count = sites * width // LANES
    got = exchange(
        jnp.concatenate(
            [
                to_tiles(tok.reshape(frames, sites, width)),
                to_tiles(grad.reshape(frames, sites, width)),
                jnp.broadcast_to(to_all, (frames,) + to_all.shape[1:]),
            ],
            axis=1,
        )
    )
    site_tok = from_tiles(got[:, :count], sites, width).reshape(length, width)
    site_grad = from_tiles(got[:, count : 2 * count], sites, width).reshape(length, width)
    at = 2 * count
    size = part * pair // LANES
    proj_full = rows_in_order(got[:, at : at + size])
    proj_full = from_tiles(proj_full.reshape(rows * frames, size, LANES), part, pair)
    proj_full = proj_full.reshape(rows, frames, part, pair).transpose(1, 0, 2, 3)
    proj_full = proj_full.reshape(width, pair)
    at += size
    size = heads * depth // LANES
    step_full = from_tiles(got[:, at : at + size], heads, depth)
    step_full = step_full.transpose(1, 0, 2).reshape(heads, width)
    at += size
    size = 2 * clips * mod_cols // LANES
    mod_full = got[:, at : at + size].reshape(frames, 2, clips, mod_cols).astype(f32)
    mod_full = (mod_full[:, 0] + mod_full[:, 1]).transpose(1, 0, 2).reshape(clips, 2 * width)
    shift, gain = mod_full[:, :width], mod_full[:, width:]

    bias = step_bias[None]
    wide = (length, width)
    site_out, site_back, gproj, gstep, site_gmod = call(
        functools.partial(site_kernel, sites),
        [(wide, bf16), (wide, bf16), ((width, pair), f32), ((heads, width), f32), ((2 * clips, width), f32)],
        [(wide, bf16)] * 2 + [((2 * length, width), bf16)],
    )(site_tok, site_grad, shift, gain, proj_full, step_full, bias, rate_time[None])

    came = exchange(
        jnp.concatenate(
            [
                to_tiles(site_out.reshape(frames, sites, width)),
                to_tiles(site_back.reshape(frames, sites, width)),
            ],
            axis=1,
        )
    )
    time_out = from_tiles(came[:, :count], sites, width).reshape(length, width)
    time_back = from_tiles(came[:, count:], sites, width).reshape(length, width)

    own_shift = lax.dynamic_slice_in_dim(shift, clip_id, 1, 0)
    own_gain = lax.dynamic_slice_in_dim(gain, clip_id, 1, 0)
    normed, coeffs, logits, inverse, decay, end_own, start_grad = call(
        band_kernel,
        [
            (wide, bf16),
            ((length, pair), bf16),
            ((length, heads), bf16),
            ((length, 1), f32),
            ((1, heads), f32),
            ((width, state), bf16),
            ((width, state), bf16),
        ],
    )(tok, grad, own_shift, own_gain, proj_full, step_full, bias, rate_space[None])
    state_in = chain(end_own, decay, True)
    later_grad = chain(start_grad, decay, False)
    mix, pre, gproj, gstep, gmod = call(
        space_kernel,
        [(wide, f32), (wide, f32), ((width, pair), bf16), ((heads, width), bf16), ((2, width), f32)],
        [(wide, bf16), ((3 * length, width), bf16)],
    )(
        tok,
        grad,
        normed,
        coeffs,
        logits,
        inverse,
        proj_full,
        step_full,
        bias,
        rate_space[None],
        skip_gain[None],
        state_in,
        later_grad,
        gproj,
        gstep,
    )

    picked = (jnp.arange(clips) == clip_id).astype(f32)[:, None]
    gmod = jnp.concatenate(
        [site_gmod[:clips] + picked * gmod[0:1], site_gmod[clips:] + picked * gmod[1:2]], axis=1
    )
    gmod = gmod.reshape(clips, frames, mod_cols).transpose(1, 0, 2).astype(bf16)
    sent = jnp.concatenate(
        [
            to_tiles(gproj.reshape(frames, depth, pair)),
            to_tiles(gstep.reshape(heads, frames, depth).transpose(1, 0, 2)),
            gmod.reshape(frames, -1, LANES) if (clips * mod_cols) % LANES == 0 else gmod,
        ],
        axis=1,
    )
    size = sent.shape[1]
    sent = jnp.pad(sent, ((0, 0), (0, -size % 8), (0, 0)))
    sums = jnp.sum(exchange(sent).astype(f32), axis=0, keepdims=True)
    sums = rows_sum(sums) * factor
    at = depth * pair // LANES
    grad_proj = from_tiles(sums[:, :at], depth, pair)[0]
    size = heads * depth // LANES
    grad_step = from_tiles(sums[:, at : at + size], heads, depth)[0].T
    at += size
    size = clips * mod_cols // LANES
    mod_sum = sums[0, at : at + size].reshape(clips, mod_cols)
    grad_mod = jnp.dot(activated.astype(f32).T, mod_sum, precision=EXACT)

    mixed, d_tokens = call(last_kernel, [(wide, bf16), (wide, bf16)])(
        tok, inverse, own_gain, mix, pre, time_out, time_back
    )
    return (mixed.reshape(tokens.shape), d_tokens.reshape(tokens.shape), grad_proj, grad_step, grad_mod)


def fits(mesh, tokens, timestep, proj_weight, step_weight):
    frames, rows = mesh.shape["frame"], mesh.shape["row"]
    length, width = tokens.shape[2] * tokens.shape[1] // rows, tokens.shape[3]
    return (
        rows == 2
        and frames == 16
        and timestep.shape[0] == 1
        and length == LANES
        and length // frames == 8
        and width // frames == LANES
        and proj_weight.shape[1] == 2 * LANES
        and step_weight.shape[1] % 32 == 0
    )


def spread_over_frames(own, radix=4):
    frames = radix * radix

    def others(piece, stride):
        return [piece] + [
            lax.ppermute(piece, "frame", [(i, i ^ (d * stride)) for i in range(frames)])
            for d in range(1, radix)
        ]

    far = jnp.stack(others(own, radix))
    return others(far, 1)


def sum_over_frames(keep, given, radix, ahead):
    frames = radix * radix

    def total(pieces):
        value = pieces[0].astype(f32)
        for piece in pieces[1:]:
            value = value + piece.astype(f32)
        return value

    def partner(piece, offset):
        return lax.ppermute(piece, "frame", [(i, i ^ offset) for i in range(frames)])

    near = [total([keep[d], given[d]]).astype(bf16) for d in range(radix)]
    near = [near[0]] + [partner(near[d], d) for d in range(1, radix)]
    near, ahead = lax.optimization_barrier((near, ahead))
    near = total(near).astype(bf16)
    far = [near[0]] + [partner(near[d], d * radix) for d in range(1, radix)]
    return total(far), *ahead


def per_device_fast(
    tokens,
    cotangent,
    timestep,
    mod_weight,
    proj_weight,
    step_weight,
    step_bias,
    rate_space,
    rate_time,
    skip_gain,
):
    frames = lax.axis_size("frame")
    rows = lax.axis_size("row")
    ids = jnp.stack([lax.axis_index("frame"), lax.axis_index("row")]).astype(jnp.int32)
    width = tokens.shape[-1]
    length = tokens.shape[1] * tokens.shape[2]
    sites = length // frames
    heads = rate_space.shape[0]
    depth, pair = proj_weight.shape
    state = pair // 2
    mod_cols = mod_weight.shape[1]
    factor = (frames * rows * length) ** (-0.5)
    tok = tokens.reshape(length, width)
    grad = cotangent.reshape(length, width)
    wide = (length, width)
    small = jnp.stack([step_bias, rate_time, rate_space, skip_gain])
    swap = [(0, 1), (1, 0)]

    packed = (frames, 2, sites, width)
    size = depth // 2 * pair // LANES + heads // 2 + 8
    activated = time_embed(timestep, mod_weight.shape[0]).astype(bf16)
    sent, payload = call(
        start_kernel,
        [(packed, bf16), ((size, LANES), bf16)],
        [
            ((depth, pair), bf16),
            ((heads, depth), bf16),
            (mod_weight.shape, bf16),
            pltpu.SemaphoreType.DMA((5,)),
        ],
        specs="shhhhhv",
    )(
        ids,
        in_hbm(tok.reshape(frames, sites, width)),
        in_hbm(grad.reshape(frames, sites, width)),
        in_hbm(proj_weight),
        in_hbm(step_weight.T),
        in_hbm(mod_weight),
        activated,
    )
    got = exchange(sent)
    payload = spread_over_frames(payload)
    other = [lax.ppermute(piece, "row", swap) for piece in payload]
    proj_full, step_full, shift, gain = call(
        functools.partial(unpack_kernel, 4),
        [((width, pair), bf16), ((heads, width), bf16), ((1, width), f32), ((1, width), f32)],
        specs="s" + "v" * 8,
    )(ids, *payload, *other)

    sent, site_x, site_gmod, site_dc, site_dl = call(
        functools.partial(site_fast_kernel, sites),
        [
            (packed, bf16),
            (wide, bf16),
            ((2, width), f32),
            ((length, pair), bf16),
            ((length, heads), bf16),
        ],
        [
            (wide, bf16),
            (packed, bf16),
            (wide, bf16),
            ((2, width), f32),
            pltpu.SemaphoreType.DMA((18,)),
        ]
        + [(wide, bf16), ((2 * length, width), bf16)],
        specs="vvvvvv",
        hbm_outs=(0, 1, 2),
    )(got, shift, gain, proj_full, step_full, small)
    sent, proj_full = lax.optimization_barrier((sent, proj_full))
    came = exchange(sent)

    normed, coeffs, logits, inverse, give = call(
        band_fast_kernel,
        [
            (wide, bf16),
            ((length, pair), bf16),
            ((length, heads), bf16),
            ((length, 1), f32),
            ((width, state), bf16),
        ],
        specs="svvvvvvv",
    )(ids, tok, grad, shift, gain, proj_full, step_full, small)
    arrived = lax.ppermute(give, "row", swap)

    mix, pre, own_dc, own_dl, gmod = call(
        space_fast_kernel,
        [(wide, f32), (wide, f32), ((length, pair), bf16), ((length, heads), bf16), ((2, width), f32)],
        [(wide, bf16), ((3 * length, width), bf16)],
        specs="s" + "v" * 10,
    )(
        ids,
        arrived,
        tok,
        grad,
        normed,
        coeffs,
        logits,
        inverse,
        proj_full,
        step_full,
        small,
    )
    pieces = call(
        functools.partial(terms_kernel, 4), [((4, size, LANES), bf16)] * 8, specs="svvvvvvvv"
    )(ids, normed, own_dc, own_dl, gmod, site_x, site_dc, site_dl, site_gmod)
    keep, given = pieces[:4], [lax.ppermute(piece, "row", swap) for piece in pieces[4:]]
    mixed, d_tokens = call(last_fast_kernel, [(wide, bf16), (wide, bf16)])(
        tok, inverse, gain, mix, pre, came
    )
    terms, mixed, d_tokens = sum_over_frames(keep, given, 4, (mixed, d_tokens))
    other = lax.ppermute(terms, "row", swap)
    (grad_mod,) = call(
        functools.partial(finish_mod_kernel, factor, size - 8),
        [((mod_weight.shape[0], mod_cols), f32)],
        specs="vv",
    )(terms, activated)
    other, grad_mod = lax.optimization_barrier((other, grad_mod))
    grad_proj, grad_step = call(
        functools.partial(finish_kernel, factor),
        [((depth, pair), f32), ((heads, depth), f32)],
        specs="svv",
    )(ids, terms, other)
    return (mixed.reshape(tokens.shape), d_tokens.reshape(tokens.shape), grad_proj, grad_step.T, grad_mod)


def solution(mesh):
    placed = (
        P("frame", "row", None, None),
        P("frame", "row", None, None),
        P(),
        P(None, "frame"),
        P("frame", None),
        P("frame", None),
        P(),
        P(),
        P(),
        P(),
    )
    outs = (
        P("frame", "row", None, None),
        P("frame", "row", None, None),
        P("frame", None),
        P("frame", None),
        P(None, "frame"),
    )

    def step(tokens, cotangent, timestep, mod_weight, proj_weight, step_weight, *rest):
        fast = fits(mesh, tokens, timestep, proj_weight, step_weight)
        body = per_device_fast if fast else per_device
        return jax.shard_map(
            body, mesh=mesh, in_specs=placed, out_specs=outs, check_vma=False
        )(tokens, cotangent, timestep, mod_weight, proj_weight, step_weight, *rest)

    return step
```

profile of v0, /device:TPU:0, one launch (start us, length us, event | category | flops | bytes accessed | tf_op | source)
XLA Modules:
  0.0 106.8 jit_solution(15070896672155987296)
XLA Ops:
  1.4 2.9 %shard_map.137 = (bf16[16,2,8,2048]{3,2,1,0:T(8,128)(2,1)}, bf16[152,128]{1,0:T(8,128)(2,1)S(1)}) custom-call(s32[2]{0:T(128)S(1)} %pad_add_fusion.ids_ref, bf16[16,8,2048]{2,1,0:T(8,128)(2,1)} %bitcast.30, bf16[16,8,2048]{2,1,0:T(8,128)(2,1)} %bitcast.34, bf16[128,256]{1,0:T(8,128)(2,1)} %proj_hbm.1, bf16[32,128]{1,0:T(8,128)(2,1)} %bitcast.41, ...), custom_call_target="tpu_custom_call" | custom-call | tf_op jit(solution)/shard_map/pallas_call | solution.py:938
  4.4 8.4 %all-to-all-start = ((bf16[16,2,8,2048]{3,2,1,0:T(8,128)(2,1)}), bf16[16,2,8,2048]{3,2,1,0:T(8,128)(2,1)S(1)}, u32[]{:S(2)}, u32[]{:S(2)}) async-start(bf16[16,2,8,2048]{3,2,1,0:T(8,128)(2,1)} %get-tuple-element.51), calls=%async_computation | async-start | bytes 2097152 | tf_op jit(solution)/shard_map/all_to_all | solution.py:44
  12.7 3.7 %collective-permute-start.2 = (bf16[152,128]{1,0:T(8,128)(2,1)S(1)}, bf16[152,128]{1,0:T(8,128)(2,1)S(1)}, u32[]{:S(2)}, u32[]{:S(2)}) collective-permute-start(bf16[152,128]{1,0:T(8,128)(2,1)S(1)} %get-tuple-element.48), channel_id=1, source_target_pairs={{0,24},{2,26},{4,28},{6,30},{8,16},{10,18},{12,20},{14,22},{16,8},... | collective-permute-start | bytes 116744 | tf_op jit(solution)/shard_map/ppermute | solution.py:878
  17.2 18.3 %collective-permute-done.2 = bf16[152,128]{1,0:T(8,128)(2,1)S(1)} collective-permute-done((bf16[152,128]{1,0:T(8,128)(2,1)S(1)}, bf16[152,128]{1,0:T(8,128)(2,1)S(1)}, u32[]{:S(2)}, u32[]{:S(2)}) %collective-permute-start.2) | collective-permute-done | bytes 38944 | tf_op jit(solution)/shard_map/ppermute | solution.py:878
  35.5 6.2 %collective-permute-done.1 = bf16[152,128]{1,0:T(8,128)(2,1)S(1)} collective-permute-done((bf16[152,128]{1,0:T(8,128)(2,1)S(1)}, bf16[152,128]{1,0:T(8,128)(2,1)S(1)}, u32[]{:S(2)}, u32[]{:S(2)}) %collective-permute-start.1) | collective-permute-done | bytes 38944 | tf_op jit(solution)/shard_map/ppermute | solution.py:878
  41.8 2.6 %collective-permute-start.5 = (bf16[4,152,128]{2,1,0:T(8,128)(2,1)S(1)}, bf16[4,152,128]{2,1,0:T(8,128)(2,1)S(1)}, u32[]{:S(2)}, u32[]{:S(2)}) collective-permute-start(bf16[4,152,128]{2,1,0:T(8,128)(2,1)S(1)} %pad_maximum_fusion.refs_0_), channel_id=1, source_target_pairs={{0,6},{2,4},{4,2},{6,0},{8,14},{10,12},{12,10},{14,8},{16,22},{18,... | collective-permute-start | bytes 466952 | tf_op jit(solution)/shard_map/ppermute | solution.py:878
  45.3 4.0 %collective-permute-done.5.refs_3_ = bf16[4,152,128]{2,1,0:T(8,128)(2,1)S(1)} collective-permute-done((bf16[4,152,128]{2,1,0:T(8,128)(2,1)S(1)}, bf16[4,152,128]{2,1,0:T(8,128)(2,1)S(1)}, u32[]{:S(2)}, u32[]{:S(2)}) %collective-permute-start.5) | collective-permute-done | bytes 155680 | tf_op jit(solution)/shard_map/ppermute | solution.py:878
  49.3 1.5 %collective-permute-done.4.refs_2_ = bf16[4,152,128]{2,1,0:T(8,128)(2,1)S(1)} collective-permute-done((bf16[4,152,128]{2,1,0:T(8,128)(2,1)S(1)}, bf16[4,152,128]{2,1,0:T(8,128)(2,1)S(1)}, u32[]{:S(2)}, u32[]{:S(2)}) %collective-permute-start.4) | collective-permute-done | bytes 155680 | tf_op jit(solution)/shard_map/ppermute | solution.py:878
  53.5 7.5 %shard_map.139 = (bf16[16,2,8,2048]{3,2,1,0:T(8,128)(2,1)}, bf16[128,2048]{1,0:T(8,128)(2,1)}, f32[2,2048]{1,0:T(2,128)}, bf16[128,256]{1,0:T(8,128)(2,1)S(1)}, bf16[128,32]{1,0:T(8,128)(2,1)S(1)}) custom-call(bf16[16,2,8,2048]{3,2,1,0:T(8,128)(2,1)S(1)} %all-to-all-done.got_ref, f32[1,2048]{1,0:T(1,128)S(1)} %get-tuple-element.49.refs_0_.refs_2_, ...), custom_call_target="tpu_custom_call" | custom-call | tf_op jit(solution)/shard_map/pallas_call | solution.py:966
  61.0 4.4 %all-to-all-start.1 = ((bf16[16,2,8,2048]{3,2,1,0:T(8,128)(2,1)}), bf16[16,2,8,2048]{3,2,1,0:T(8,128)(2,1)S(1)}, u32[]{:S(2)}, u32[]{:S(2)}) async-start(bf16[16,2,8,2048]{3,2,1,0:T(8,128)(2,1)} %get-tuple-element.78), calls=%async_computation.1 | async-start | bytes 2097152 | tf_op jit(solution)/shard_map/all_to_all | solution.py:44
  65.4 2.0 %shard_map.140 = (bf16[128,2048]{1,0:T(8,128)(2,1)S(1)}, bf16[128,256]{1,0:T(8,128)(2,1)S(1)}, bf16[128,32]{1,0:T(8,128)(2,1)S(1)}, f32[128,1]{1,0:T(8,128)S(1)}, bf16[2048,128]{1,0:T(8,128)(2,1)S(1)}) custom-call(s32[2]{0:T(128)S(1)} %pad_add_fusion.ids_ref, bf16[128,2048]{1,0:T(8,128)(2,1)S(1)} %bitcast.31, bf16[128,2048]{1,0:T(8,128)(2,1)S(1)} %bitcast.35, ...), custom_call_target="tpu_custom_call" | custom-call | tf_op jit(solution)/shard_map/pallas_call | solution.py:989
  67.5 1.9 %collective-permute-done.10.arrived_ref = bf16[2048,128]{1,0:T(8,128)(2,1)S(1)} collective-permute-done((bf16[2048,128]{1,0:T(8,128)(2,1)S(1)}, bf16[2048,128]{1,0:T(8,128)(2,1)S(1)}, u32[]{:S(2)}, u32[]{:S(2)}) %collective-permute-start.10) | collective-permute-done | bytes 524320 | tf_op jit(solution)/shard_map/ppermute | solution.py:1000
  69.4 6.8 %shard_map.141 = (f32[128,2048]{1,0:T(8,128)S(1)}, f32[128,2048]{1,0:T(8,128)S(1)}, bf16[128,256]{1,0:T(8,128)(2,1)S(1)}, bf16[128,32]{1,0:T(8,128)(2,1)S(1)}, f32[2,2048]{1,0:T(2,128)S(1)}) custom-call(s32[2]{0:T(128)S(1)} %pad_add_fusion.ids_ref, bf16[2048,128]{1,0:T(8,128)(2,1)S(1)} %collective-permute-done.10.arrived_ref, ...), custom_call_target="tpu_custom_call" | custom-call | tf_op jit(solution)/shard_map/pallas_call | solution.py:1002
  76.3 1.3 %shard_map.142 = (bf16[4,152,128]{2,1,0:T(8,128)(2,1)S(1)}, bf16[4,152,128]{2,1,0:T(8,128)(2,1)S(1)}, bf16[4,152,128]{2,1,0:T(8,128)(2,1)S(1)}, bf16[4,152,128]{...) custom-call(s32[2]{0:T(128)S(1)} %pad_add_fusion.ids_ref, ...), custom_call_target="tpu_custom_call" | custom-call | tf_op jit(solution)/shard_map/pallas_call | solution.py:1020
  79.1 2.0 %collective-permute-start.13 = (bf16[4,152,128]{2,1,0:T(8,128)(2,1)S(1)}, bf16[4,152,128]{2,1,0:T(8,128)(2,1)S(1)}, u32[]{:S(2)}, u32[]{:S(2)}) collective-permute-start(bf16[4,152,128]{2,1,0:T(8,128)(2,1)S(1)} %add_convert_fusion.3), channel_id=1, source_target_pairs={{0,2},{2,0},{4,6},{6,4},{8,10},{10,8},{12,14},{14,12},{16,18},{18,... | collective-permute-start | bytes 466952 | tf_op jit(solution)/shard_map/ppermute | solution.py:896
  81.1 1.5 %collective-permute-start.15 = (bf16[4,152,128]{2,1,0:T(8,128)(2,1)S(1)}, bf16[4,152,128]{2,1,0:T(8,128)(2,1)S(1)}, u32[]{:S(2)}, u32[]{:S(2)}) collective-permute-start(bf16[4,152,128]{2,1,0:T(8,128)(2,1)S(1)} %add_convert_fusion.2), channel_id=1, source_target_pairs={{0,4},{2,6},{4,0},{6,2},{8,12},{10,14},{12,8},{14,10},{16,20},{18,... | collective-permute-start | bytes 466952 | tf_op jit(solution)/shard_map/ppermute | solution.py:896
  83.2 6.8 %all-to-all-done.1.came_ref = bf16[16,2,8,2048]{3,2,1,0:T(8,128)(2,1)S(1)} async-done(((bf16[16,2,8,2048]{3,2,1,0:T(8,128)(2,1)}), bf16[16,2,8,2048]{3,2,1,0:T(8,128)(2,1)S(1)}, u32[]{:S(2)}, u32[]{:S(2)}) %all-to-all-start.1) | async-done | bytes 1048608 | tf_op jit(solution)/shard_map/all_to_all | solution.py:44
  90.1 1.2 %copy-done.3 = f32[128,2048]{1,0:T(8,128)S(1)} copy-done((f32[128,2048]{1,0:T(8,128)S(1)}, f32[128,2048]{1,0:T(8,128)}, u32[]{:S(2)}) %copy-start.3) | copy-done | bytes 1048600
  91.3 1.2 %copy-done.5 = f32[128,2048]{1,0:T(8,128)S(1)} copy-done((f32[128,2048]{1,0:T(8,128)S(1)}, f32[128,2048]{1,0:T(8,128)}, u32[]{:S(2)}) %copy-start.5) | copy-done | bytes 1048600
  92.5 1.7 %shard_map.143 = (bf16[128,2048]{1,0:T(8,128)(2,1)}, bf16[128,2048]{1,0:T(8,128)(2,1)}) custom-call(bf16[128,2048]{1,0:T(8,128)(2,1)S(1)} %bitcast.33, f32[128,1]{1,0:T(8,128)S(1)} %get-tuple-element.60.refs_5_.inverse_ref, f32[1,2048]{1,0:T(1,128)S(1)} %get-tuple-element.50.refs_1_.refs_3_.gain_ref, f32[128,2048]{1,0:T(8,128)S(1)} %copy-done.3, ...), custom_call_target="tpu_custom_call" | custom-call | tf_op jit(solution)/shard_map/pallas_call | solution.py:1024
  94.3 3.3 %collective-permute-start.18 = (bf16[152,128]{1,0:T(8,128)(2,1)S(1)}, bf16[152,128]{1,0:T(8,128)(2,1)S(1)}, u32[]{:S(2)}, u32[]{:S(2)}) collective-permute-start(bf16[152,128]{1,0:T(8,128)(2,1)S(1)} %get-tuple-element.91), channel_id=1, source_target_pairs={{0,8},{2,10},{4,12},{6,14},{8,0},{10,2},{12,4},{14,6},{16,24},{18,... | collective-permute-start | bytes 116744 | tf_op jit(solution)/shard_map/ppermute | solution.py:896
  97.6 1.4 %collective-permute-start.20 = (bf16[152,128]{1,0:T(8,128)(2,1)S(1)}, bf16[152,128]{1,0:T(8,128)(2,1)S(1)}, u32[]{:S(2)}, u32[]{:S(2)}) collective-permute-start(bf16[152,128]{1,0:T(8,128)(2,1)S(1)} %get-tuple-element.92), channel_id=1, source_target_pairs={{0,24},{2,26},{4,28},{6,30},{8,16},{10,18},{12,20},{14,22},{16,8},... | collective-permute-start | bytes 116744 | tf_op jit(solution)/shard_map/ppermute | solution.py:896
  99.6 3.8 %collective-permute-done.20 = bf16[152,128]{1,0:T(8,128)(2,1)S(1)} collective-permute-done((bf16[152,128]{1,0:T(8,128)(2,1)S(1)}, bf16[152,128]{1,0:T(8,128)(2,1)S(1)}, u32[]{:S(2)}, u32[]{:S(2)}) %collective-permute-start.20) | collective-permute-done | bytes 38944 | tf_op jit(solution)/shard_map/ppermute | solution.py:896
  105.6 1.2 %shard_map.145 = (f32[128,256]{1,0:T(8,128)}, f32[32,128]{1,0:T(8,128)}) custom-call(s32[2]{0:T(128)S(1)} %pad_add_fusion.ids_ref, f32[152,128]{1,0:T(8,128)S(1)} %fusion.1.sums_ref.own_ref, f32[152,128]{1,0:T(8,128)S(1)} %collective-permute-done.21.other_ref), custom_call_target="tpu_custom_call" | custom-call | tf_op jit(solution)/shard_map/pallas_call | solution.py:1035
  (68 shorter events, 9.6 us)
Async XLA Ops:
  4.4 49.1 %all-to-all-start = ((bf16[16,2,8,2048]{3,2,1,0:T(8,128)(2,1)}), bf16[16,2,8,2048]{3,2,1,0:T(8,128)(2,1)S(1)}, u32[]{:S(2)}, u32[]{:S(2)}) async-start(bf16[16,2,8,2048]{3,2,1,0:T(8,128)(2,1)} %get-tuple-element.51), calls=%async_computation | async-start | bytes 2097152 | tf_op jit(solution)/shard_map/all_to_all | solution.py:44
  12.7 22.8 %collective-permute-start.2 = (bf16[152,128]{1,0:T(8,128)(2,1)S(1)}, bf16[152,128]{1,0:T(8,128)(2,1)S(1)}, u32[]{:S(2)}, u32[]{:S(2)}) collective-permute-start(bf16[152,128]{1,0:T(8,128)(2,1)S(1)} %get-tuple-element.48), channel_id=1, source_target_pairs={{0,24},{2,26},{4,28},{6,30},{8,16},{10,18},{12,20},{14,22},{16,8},... | collective-permute-start | bytes 116744 | tf_op jit(solution)/shard_map/ppermute | solution.py:878
  16.4 25.3 %collective-permute-start.1 = (bf16[152,128]{1,0:T(8,128)(2,1)S(1)}, bf16[152,128]{1,0:T(8,128)(2,1)S(1)}, u32[]{:S(2)}, u32[]{:S(2)}) collective-permute-start(bf16[152,128]{1,0:T(8,128)(2,1)S(1)} %get-tuple-element.48), channel_id=1, source_target_pairs={{0,16},{2,18},{4,20},{6,22},{8,24},{10,26},{12,28},{14,30},{16,0},... | collective-permute-start | bytes 116744 | tf_op jit(solution)/shard_map/ppermute | solution.py:878
  16.4 25.3 %collective-permute-start = (bf16[152,128]{1,0:T(8,128)(2,1)S(1)}, bf16[152,128]{1,0:T(8,128)(2,1)S(1)}, u32[]{:S(2)}, u32[]{:S(2)}) collective-permute-start(bf16[152,128]{1,0:T(8,128)(2,1)S(1)} %get-tuple-element.48), channel_id=1, source_target_pairs={{0,8},{2,10},{4,12},{6,14},{8,0},{10,2},{12,4},{14,6},{16,24},{18,... | collective-permute-start | bytes 116744 | tf_op jit(solution)/shard_map/ppermute | solution.py:878
  41.8 7.5 %collective-permute-start.5 = (bf16[4,152,128]{2,1,0:T(8,128)(2,1)S(1)}, bf16[4,152,128]{2,1,0:T(8,128)(2,1)S(1)}, u32[]{:S(2)}, u32[]{:S(2)}) collective-permute-start(bf16[4,152,128]{2,1,0:T(8,128)(2,1)S(1)} %pad_maximum_fusion.refs_0_), channel_id=1, source_target_pairs={{0,6},{2,4},{4,2},{6,0},{8,14},{10,12},{12,10},{14,8},{16,22},{18,... | collective-permute-start | bytes 466952 | tf_op jit(solution)/shard_map/ppermute | solution.py:878
  44.3 6.5 %collective-permute-start.4 = (bf16[4,152,128]{2,1,0:T(8,128)(2,1)S(1)}, bf16[4,152,128]{2,1,0:T(8,128)(2,1)S(1)}, u32[]{:S(2)}, u32[]{:S(2)}) collective-permute-start(bf16[4,152,128]{2,1,0:T(8,128)(2,1)S(1)} %pad_maximum_fusion.refs_0_), channel_id=1, source_target_pairs={{0,4},{2,6},{4,0},{6,2},{8,12},{10,14},{12,8},{14,10},{16,20},{18,... | collective-permute-start | bytes 466952 | tf_op jit(solution)/shard_map/ppermute | solution.py:878
  44.7 6.2 %collective-permute-start.3 = (bf16[4,152,128]{2,1,0:T(8,128)(2,1)S(1)}, bf16[4,152,128]{2,1,0:T(8,128)(2,1)S(1)}, u32[]{:S(2)}, u32[]{:S(2)}) collective-permute-start(bf16[4,152,128]{2,1,0:T(8,128)(2,1)S(1)} %pad_maximum_fusion.refs_0_), channel_id=1, source_target_pairs={{0,2},{2,0},{4,6},{6,4},{8,10},{10,8},{12,14},{14,12},{16,18},{18,... | collective-permute-start | bytes 466952 | tf_op jit(solution)/shard_map/ppermute | solution.py:878
  45.3 6.7 %collective-permute-start.6 = (bf16[4,152,128]{2,1,0:T(8,128)(2,1)S(1)}, bf16[4,152,128]{2,1,0:T(8,128)(2,1)S(1)}, u32[]{:S(2)}, u32[]{:S(2)}) collective-permute-start(bf16[4,152,128]{2,1,0:T(8,128)(2,1)S(1)} %pad_maximum_fusion.refs_0_), channel_id=1, source_target_pairs={{0,1},{1,0},{2,3},{3,2},{4,5},{5,4},{6,7},{7,6},{8,9},{9,8},{10,11... | collective-permute-start | bytes 466952 | tf_op jit(solution)/shard_map/ppermute | solution.py:959
  49.3 2.8 %collective-permute-start.9 = (bf16[4,152,128]{2,1,0:T(8,128)(2,1)S(1)}, bf16[4,152,128]{2,1,0:T(8,128)(2,1)S(1)}, u32[]{:S(2)}, u32[]{:S(2)}) collective-permute-start(bf16[4,152,128]{2,1,0:T(8,128)(2,1)S(1)} %collective-permute-done.5.refs_3_), channel_id=1, source_target_pairs={{0,1},{1,0},{2,3},{3,2},{4,5},{5,4},{6,7},{7,6},{8,9},{9,8},{10,11... | collective-permute-start | bytes 466952 | tf_op jit(solution)/shard_map/ppermute | solution.py:959
  50.8 1.4 %collective-permute-start.8 = (bf16[4,152,128]{2,1,0:T(8,128)(2,1)S(1)}, bf16[4,152,128]{2,1,0:T(8,128)(2,1)S(1)}, u32[]{:S(2)}, u32[]{:S(2)}) collective-permute-start(bf16[4,152,128]{2,1,0:T(8,128)(2,1)S(1)} %collective-permute-done.4.refs_2_), channel_id=1, source_target_pairs={{0,1},{1,0},{2,3},{3,2},{4,5},{5,4},{6,7},{7,6},{8,9},{9,8},{10,11... | collective-permute-start | bytes 466952 | tf_op jit(solution)/shard_map/ppermute | solution.py:959
  50.9 1.5 %collective-permute-start.7 = (bf16[4,152,128]{2,1,0:T(8,128)(2,1)S(1)}, bf16[4,152,128]{2,1,0:T(8,128)(2,1)S(1)}, u32[]{:S(2)}, u32[]{:S(2)}) collective-permute-start(bf16[4,152,128]{2,1,0:T(8,128)(2,1)S(1)} %collective-permute-done.3.refs_1_), channel_id=1, source_target_pairs={{0,1},{1,0},{2,3},{3,2},{4,5},{5,4},{6,7},{7,6},{8,9},{9,8},{10,11... | collective-permute-start | bytes 466952 | tf_op jit(solution)/shard_map/ppermute | solution.py:959
  61.0 29.1 %all-to-all-start.1 = ((bf16[16,2,8,2048]{3,2,1,0:T(8,128)(2,1)}), bf16[16,2,8,2048]{3,2,1,0:T(8,128)(2,1)S(1)}, u32[]{:S(2)}, u32[]{:S(2)}) async-start(bf16[16,2,8,2048]{3,2,1,0:T(8,128)(2,1)} %get-tuple-element.78), calls=%async_computation.1 | async-start | bytes 2097152 | tf_op jit(solution)/shard_map/all_to_all | solution.py:44
  67.4 2.0 %collective-permute-start.10 = (bf16[2048,128]{1,0:T(8,128)(2,1)S(1)}, bf16[2048,128]{1,0:T(8,128)(2,1)S(1)}, u32[]{:S(2)}, u32[]{:S(2)}) collective-permute-start(bf16[2048,128]{1,0:T(8,128)(2,1)S(1)} %get-tuple-element.57), channel_id=1, source_target_pairs={{0,1},{1,0},{2,3},{3,2},{4,5},{5,4},{6,7},{7,6},{8,9},{9,8},{10,11... | collective-permute-start | bytes 1572872 | tf_op jit(solution)/shard_map/ppermute | solution.py:1000
  77.6 1.4 %collective-permute-start.12 = (bf16[4,152,128]{2,1,0:T(8,128)(2,1)S(1)}, bf16[4,152,128]{2,1,0:T(8,128)(2,1)S(1)}, u32[]{:S(2)}, u32[]{:S(2)}) collective-permute-start(bf16[4,152,128]{2,1,0:T(8,128)(2,1)S(1)} %get-tuple-element.71), channel_id=1, source_target_pairs={{0,1},{1,0},{2,3},{3,2},{4,5},{5,4},{6,7},{7,6},{8,9},{9,8},{10,11... | collective-permute-start | bytes 466952 | tf_op jit(solution)/shard_map/ppermute | solution.py:1023
  77.8 5.4 %collective-permute-start.11 = (bf16[4,152,128]{2,1,0:T(8,128)(2,1)S(1)}, bf16[4,152,128]{2,1,0:T(8,128)(2,1)S(1)}, u32[]{:S(2)}, u32[]{:S(2)}) collective-permute-start(bf16[4,152,128]{2,1,0:T(8,128)(2,1)S(1)} %get-tuple-element.69), channel_id=1, source_target_pairs={{0,1},{1,0},{2,3},{3,2},{4,5},{5,4},{6,7},{7,6},{8,9},{9,8},{10,11... | collective-permute-start | bytes 466952 | tf_op jit(solution)/shard_map/ppermute | solution.py:1023
  78.2 2.9 %collective-permute-start.14 = (bf16[4,152,128]{2,1,0:T(8,128)(2,1)S(1)}, bf16[4,152,128]{2,1,0:T(8,128)(2,1)S(1)}, u32[]{:S(2)}, u32[]{:S(2)}) collective-permute-start(bf16[4,152,128]{2,1,0:T(8,128)(2,1)S(1)} %get-tuple-element.73), channel_id=1, source_target_pairs={{0,1},{1,0},{2,3},{3,2},{4,5},{5,4},{6,7},{7,6},{8,9},{9,8},{10,11... | collective-permute-start | bytes 466952 | tf_op jit(solution)/shard_map/ppermute | solution.py:1023
  78.3 4.4 %collective-permute-start.16 = (bf16[4,152,128]{2,1,0:T(8,128)(2,1)S(1)}, bf16[4,152,128]{2,1,0:T(8,128)(2,1)S(1)}, u32[]{:S(2)}, u32[]{:S(2)}) collective-permute-start(bf16[4,152,128]{2,1,0:T(8,128)(2,1)S(1)} %get-tuple-element.75), channel_id=1, source_target_pairs={{0,1},{1,0},{2,3},{3,2},{4,5},{5,4},{6,7},{7,6},{8,9},{9,8},{10,11... | collective-permute-start | bytes 466952 | tf_op jit(solution)/shard_map/ppermute | solution.py:1023
  79.1 15.1 %collective-permute-start.13 = (bf16[4,152,128]{2,1,0:T(8,128)(2,1)S(1)}, bf16[4,152,128]{2,1,0:T(8,128)(2,1)S(1)}, u32[]{:S(2)}, u32[]{:S(2)}) collective-permute-start(bf16[4,152,128]{2,1,0:T(8,128)(2,1)S(1)} %add_convert_fusion.3), channel_id=1, source_target_pairs={{0,2},{2,0},{4,6},{6,4},{8,10},{10,8},{12,14},{14,12},{16,18},{18,... | collective-permute-start | bytes 466952 | tf_op jit(solution)/shard_map/ppermute | solution.py:896
  81.1 13.1 %collective-permute-start.15 = (bf16[4,152,128]{2,1,0:T(8,128)(2,1)S(1)}, bf16[4,152,128]{2,1,0:T(8,128)(2,1)S(1)}, u32[]{:S(2)}, u32[]{:S(2)}) collective-permute-start(bf16[4,152,128]{2,1,0:T(8,128)(2,1)S(1)} %add_convert_fusion.2), channel_id=1, source_target_pairs={{0,4},{2,6},{4,0},{6,2},{8,12},{10,14},{12,8},{14,10},{16,20},{18,... | collective-permute-start | bytes 466952 | tf_op jit(solution)/shard_map/ppermute | solution.py:896
  82.7 11.5 %collective-permute-start.17 = (bf16[4,152,128]{2,1,0:T(8,128)(2,1)S(1)}, bf16[4,152,128]{2,1,0:T(8,128)(2,1)S(1)}, u32[]{:S(2)}, u32[]{:S(2)}) collective-permute-start(bf16[4,152,128]{2,1,0:T(8,128)(2,1)S(1)} %add_convert_fusion.1), channel_id=1, source_target_pairs={{0,6},{2,4},{4,2},{6,0},{8,14},{10,12},{12,10},{14,8},{16,22},{18,... | collective-permute-start | bytes 466952 | tf_op jit(solution)/shard_map/ppermute | solution.py:896
  94.3 5.3 %collective-permute-start.18 = (bf16[152,128]{1,0:T(8,128)(2,1)S(1)}, bf16[152,128]{1,0:T(8,128)(2,1)S(1)}, u32[]{:S(2)}, u32[]{:S(2)}) collective-permute-start(bf16[152,128]{1,0:T(8,128)(2,1)S(1)} %get-tuple-element.91), channel_id=1, source_target_pairs={{0,8},{2,10},{4,12},{6,14},{8,0},{10,2},{12,4},{14,6},{16,24},{18,... | collective-permute-start | bytes 116744 | tf_op jit(solution)/shard_map/ppermute | solution.py:896
  97.6 5.8 %collective-permute-start.20 = (bf16[152,128]{1,0:T(8,128)(2,1)S(1)}, bf16[152,128]{1,0:T(8,128)(2,1)S(1)}, u32[]{:S(2)}, u32[]{:S(2)}) collective-permute-start(bf16[152,128]{1,0:T(8,128)(2,1)S(1)} %get-tuple-element.92), channel_id=1, source_target_pairs={{0,24},{2,26},{4,28},{6,30},{8,16},{10,18},{12,20},{14,22},{16,8},... | collective-permute-start | bytes 116744 | tf_op jit(solution)/shard_map/ppermute | solution.py:896
  99.0 5.2 %collective-permute-start.19 = (bf16[152,128]{1,0:T(8,128)(2,1)S(1)}, bf16[152,128]{1,0:T(8,128)(2,1)S(1)}, u32[]{:S(2)}, u32[]{:S(2)}) collective-permute-start(bf16[152,128]{1,0:T(8,128)(2,1)S(1)} %get-tuple-element.93), channel_id=1, source_target_pairs={{0,16},{2,18},{4,20},{6,22},{8,24},{10,26},{12,28},{14,30},{16,0},... | collective-permute-start | bytes 116744 | tf_op jit(solution)/shard_map/ppermute | solution.py:896
  104.3 1.3 %collective-permute-start.21 = (f32[152,128]{1,0:T(8,128)S(1)}, f32[152,128]{1,0:T(8,128)S(1)}, u32[]{:S(2)}, u32[]{:S(2)}) collective-permute-start(f32[152,128]{1,0:T(8,128)S(1)} %fusion.1.sums_ref.own_ref), channel_id=1, source_target_pairs={{0,1},{1,0},{2,3},{3,2},{4,5},{5,4},{6,7},{7,6},{8,9},{9,8},{10,11... | collective-permute-start | bytes 233480 | tf_op jit(solution)/shard_map/ppermute | solution.py:1028
  (12 other events, 46.3 us)
where the time goes:
time: 107 us
  waiting for transfers between devices  44.8 us (42%)
  starting transfers between devices  31.2 us (29%)
  Pallas kernels  25.6 us (24%)
  local copies, waits for them, and re-layouts  3.17 us (3%)
  between operations  1.53 us (1%)
    ppermute x6, waiting for transfers between devices, others(): lax.ppermute(piece, 'frame', [(i, i ^ d * stride) for i in range(frames)])  30.2 us
    all_to_all x2, starting transfers between devices, exchange(): lax.all_to_all(packed, 'frame', split_axis=0, concat_axis=0, tiled=True)  12.7 us
    ppermute x6, starting transfers between devices, partner(): lax.ppermute(piece, 'frame', [(i, i ^ offset) for i in range(frames)])  8.79 us
    ppermute x6, starting transfers between devices, others(): lax.ppermute(piece, 'frame', [(i, i ^ d * stride) for i in range(frames)])  8.01 us
    pallas_call x1, Pallas kernels, per_device_fast(): call(functools.partial(site_fast_kernel, sites), [(packed, bf16), (wide,...  7.49 us
    pallas_call x1, Pallas kernels, per_device_fast(): call(space_fast_kernel, [(wide, f32), (wide, f32), ((length, pair), bf16)...  6.84 us
    all_to_all x2, waiting for transfers between devices, exchange(): lax.all_to_all(packed, 'frame', split_axis=0, concat_axis=0, tiled=True)  6.83 us
    ppermute x6, waiting for transfers between devices, partner(): lax.ppermute(piece, 'frame', [(i, i ^ offset) for i in range(frames)])  5.08 us
  transfers between devices with their start and end apart: 24, of which 14 were waited for; matrix products, arithmetic and copies ran while one was open for 0% of the time, Pallas kernels for 13%

commit v1 on v0

--- a/solution.py
+++ b/solution.py
@@ -146,11 +146,12 @@
     grads = jnp.concatenate([jnp.where(own, grad, zero) for own in inside], axis=0)
     d_weights = mm(grads, stepped, 1, 1)
     weights = []
+    low_scores = scores.astype(bf16)
     for i in range(per_block):
         h = j * per_block + i
         decay = jnp.exp2(jnp.minimum(cums[0][:, h : h + 1] - cums[1][h : h + 1, :], 0.0))
         d_scores = d_scores + d_weights[i * length : (i + 1) * length] * decay
-        weights.append((scores * decay).astype(bf16))
+        weights.append(low_scores * decay.astype(bf16))
     out = mm(jnp.concatenate(weights, axis=1), steppeds, 1, 0)
     d_stepped = mm(jnp.concatenate(weights, axis=0), grads, 0, 0)
     return stepped, out, d_stepped, d_scores
@@ -370,20 +371,18 @@
     d_coeffs = jnp.concatenate(
         [mm(d_scores, c_part, 0, 0), mm(d_scores, b_part, 1, 0)], axis=1
     ).astype(bf16)
-    clip = lax.broadcasted_iota(jnp.int32, (8, length), 1) // (length // clips)
-    clip_row = lax.broadcasted_iota(jnp.int32, (8, length), 0)
-    pick = jnp.where(clip == clip_row, 1.0, 0.0).astype(bf16)
     for sl in wide_blocks(width):
         back = (
             dn_ref[:, sl].astype(f32)
             + mm(d_coeffs, proj_ref[sl, :], 1, 1)
             + mm(d_logits, step_ref[:, sl], 1, 0)
         )
-        low = back.astype(bf16)
-        back_ref[:, sl] = low
-        scaled = (back * (tok_ref[:, sl].astype(f32) * inverse)).astype(bf16)
-        gmod_ref[0:clips, sl] = mm(pick, low, 1, 0)[0:clips]
-        gmod_ref[clips : 2 * clips, sl] = mm(pick, scaled, 1, 0)[0:clips]
+        back_ref[:, sl] = back.astype(bf16)
+        scaled = back * (tok_ref[:, sl].astype(f32) * inverse)
+        for c in range(clips):
+            rows = slice(c * (length // clips), (c + 1) * (length // clips))
+            gmod_ref[c : c + 1, sl] = jnp.sum(back[rows], axis=0, keepdims=True)
+            gmod_ref[clips + c : clips + c + 1, sl] = jnp.sum(scaled[rows], axis=0, keepdims=True)
         if gproj_ref.shape == (width, 2 * state):
             gproj_ref[sl, :] = mm(x_ref[:, sl], d_coeffs, 0, 0)
             gstep_ref[:, sl] = mm(d_logits, x_ref[:, sl], 0, 0)

time: 107 us -> 106 us (level)
  Pallas kernels: 25.6 us -> 24.5 us
    pallas_call x1, Pallas kernels: 7.49 us -> 6.41 us  [per_device_fast(): call(functools.partial(site_fast_kernel, sites), [(packed, bf16), (wide,...]
where the time goes in v1:
time: 106 us
  waiting for transfers between devices  44.8 us (42%)
  starting transfers between devices  31.2 us (29%)
  Pallas kernels  24.5 us (23%)
  local copies, waits for them, and re-layouts  3.17 us (3%)
  between operations  1.53 us (1%)
    ppermute x6, waiting for transfers between devices, others(): lax.ppermute(piece, 'frame', [(i, i ^ d * stride) for i in range(frames)])  30.2 us
    all_to_all x2, starting transfers between devices, exchange(): lax.all_to_all(packed, 'frame', split_axis=0, concat_axis=0, tiled=True)  12.7 us
    ppermute x6, starting transfers between devices, partner(): lax.ppermute(piece, 'frame', [(i, i ^ offset) for i in range(frames)])  8.81 us
    ppermute x6, starting transfers between devices, others(): lax.ppermute(piece, 'frame', [(i, i ^ d * stride) for i in range(frames)])  8.01 us
    all_to_all x2, waiting for transfers between devices, exchange(): lax.all_to_all(packed, 'frame', split_axis=0, concat_axis=0, tiled=True)  6.84 us
    pallas_call x1, Pallas kernels, per_device_fast(): call(space_fast_kernel, [(wide, f32), (wide, f32), ((length, pair), bf16)...  6.83 us
    pallas_call x1, Pallas kernels, per_device_fast(): call(functools.partial(site_fast_kernel, sites), [(packed, bf16), (wide,...  6.41 us
    ppermute x6, waiting for transfers between devices, partner(): lax.ppermute(piece, 'frame', [(i, i ^ offset) for i in range(frames)])  5.08 us
  transfers between devices with their start and end apart: 24, of which 14 were waited for; matrix products, arithmetic and copies ran while one was open for 0% of the time, Pallas kernels for 13%

profile of v1, /device:TPU:0, one launch (start us, length us, event | category | flops | bytes accessed | tf_op | source)
XLA Modules:
  0.0 105.7 jit_solution(636453442475828746)
XLA Ops:
  1.4 2.9 %shard_map.137 = (bf16[16,2,8,2048]{3,2,1,0:T(8,128)(2,1)}, bf16[152,128]{1,0:T(8,128)(2,1)S(1)}) custom-call(s32[2]{0:T(128)S(1)} %pad_add_fusion.ids_ref, bf16[16,8,2048]{2,1,0:T(8,128)(2,1)} %bitcast.30, bf16[16,8,2048]{2,1,0:T(8,128)(2,1)} %bitcast.34, bf16[128,256]{1,0:T(8,128)(2,1)} %proj_hbm.1, bf16[32,128]{1,0:T(8,128)(2,1)} %bitcast.41, ...), custom_call_target="tpu_custom_call" | custom-call | tf_op jit(solution)/shard_map/pallas_call | solution.py:937
  4.4 8.4 %all-to-all-start = ((bf16[16,2,8,2048]{3,2,1,0:T(8,128)(2,1)}), bf16[16,2,8,2048]{3,2,1,0:T(8,128)(2,1)S(1)}, u32[]{:S(2)}, u32[]{:S(2)}) async-start(bf16[16,2,8,2048]{3,2,1,0:T(8,128)(2,1)} %get-tuple-element.51), calls=%async_computation | async-start | bytes 2097152 | tf_op jit(solution)/shard_map/all_to_all | solution.py:44
  12.7 3.7 %collective-permute-start.2 = (bf16[152,128]{1,0:T(8,128)(2,1)S(1)}, bf16[152,128]{1,0:T(8,128)(2,1)S(1)}, u32[]{:S(2)}, u32[]{:S(2)}) collective-permute-start(bf16[152,128]{1,0:T(8,128)(2,1)S(1)} %get-tuple-element.48), channel_id=1, source_target_pairs={{0,24},{2,26},{4,28},{6,30},{8,16},{10,18},{12,20},{14,22},{16,8},... | collective-permute-start | bytes 116744 | tf_op jit(solution)/shard_map/ppermute | solution.py:877
  17.2 18.3 %collective-permute-done.2 = bf16[152,128]{1,0:T(8,128)(2,1)S(1)} collective-permute-done((bf16[152,128]{1,0:T(8,128)(2,1)S(1)}, bf16[152,128]{1,0:T(8,128)(2,1)S(1)}, u32[]{:S(2)}, u32[]{:S(2)}) %collective-permute-start.2) | collective-permute-done | bytes 38944 | tf_op jit(solution)/shard_map/ppermute | solution.py:877
  35.5 6.2 %collective-permute-done.1 = bf16[152,128]{1,0:T(8,128)(2,1)S(1)} collective-permute-done((bf16[152,128]{1,0:T(8,128)(2,1)S(1)}, bf16[152,128]{1,0:T(8,128)(2,1)S(1)}, u32[]{:S(2)}, u32[]{:S(2)}) %collective-permute-start.1) | collective-permute-done | bytes 38944 | tf_op jit(solution)/shard_map/ppermute | solution.py:877
  41.8 2.6 %collective-permute-start.5 = (bf16[4,152,128]{2,1,0:T(8,128)(2,1)S(1)}, bf16[4,152,128]{2,1,0:T(8,128)(2,1)S(1)}, u32[]{:S(2)}, u32[]{:S(2)}) collective-permute-start(bf16[4,152,128]{2,1,0:T(8,128)(2,1)S(1)} %pad_maximum_fusion.refs_0_), channel_id=1, source_target_pairs={{0,6},{2,4},{4,2},{6,0},{8,14},{10,12},{12,10},{14,8},{16,22},{18,... | collective-permute-start | bytes 466952 | tf_op jit(solution)/shard_map/ppermute | solution.py:877
  45.3 4.0 %collective-permute-done.5.refs_3_ = bf16[4,152,128]{2,1,0:T(8,128)(2,1)S(1)} collective-permute-done((bf16[4,152,128]{2,1,0:T(8,128)(2,1)S(1)}, bf16[4,152,128]{2,1,0:T(8,128)(2,1)S(1)}, u32[]{:S(2)}, u32[]{:S(2)}) %collective-permute-start.5) | collective-permute-done | bytes 155680 | tf_op jit(solution)/shard_map/ppermute | solution.py:877
  49.3 1.5 %collective-permute-done.4.refs_2_ = bf16[4,152,128]{2,1,0:T(8,128)(2,1)S(1)} collective-permute-done((bf16[4,152,128]{2,1,0:T(8,128)(2,1)S(1)}, bf16[4,152,128]{2,1,0:T(8,128)(2,1)S(1)}, u32[]{:S(2)}, u32[]{:S(2)}) %collective-permute-start.4) | collective-permute-done | bytes 155680 | tf_op jit(solution)/shard_map/ppermute | solution.py:877
  53.5 6.4 %shard_map.139 = (bf16[16,2,8,2048]{3,2,1,0:T(8,128)(2,1)}, bf16[128,2048]{1,0:T(8,128)(2,1)}, f32[2,2048]{1,0:T(2,128)}, bf16[128,256]{1,0:T(8,128)(2,1)S(1)}, bf16[128,32]{1,0:T(8,128)(2,1)S(1)}) custom-call(bf16[16,2,8,2048]{3,2,1,0:T(8,128)(2,1)S(1)} %all-to-all-done.got_ref, f32[1,2048]{1,0:T(1,128)S(1)} %get-tuple-element.49.refs_0_.refs_2_, ...), custom_call_target="tpu_custom_call" | custom-call | tf_op jit(solution)/shard_map/pallas_call | solution.py:965
  59.9 4.4 %all-to-all-start.1 = ((bf16[16,2,8,2048]{3,2,1,0:T(8,128)(2,1)}), bf16[16,2,8,2048]{3,2,1,0:T(8,128)(2,1)S(1)}, u32[]{:S(2)}, u32[]{:S(2)}) async-start(bf16[16,2,8,2048]{3,2,1,0:T(8,128)(2,1)} %get-tuple-element.78), calls=%async_computation.1 | async-start | bytes 2097152 | tf_op jit(solution)/shard_map/all_to_all | solution.py:44
  64.3 2.0 %shard_map.140 = (bf16[128,2048]{1,0:T(8,128)(2,1)S(1)}, bf16[128,256]{1,0:T(8,128)(2,1)S(1)}, bf16[128,32]{1,0:T(8,128)(2,1)S(1)}, f32[128,1]{1,0:T(8,128)S(1)}, bf16[2048,128]{1,0:T(8,128)(2,1)S(1)}) custom-call(s32[2]{0:T(128)S(1)} %pad_add_fusion.ids_ref, bf16[128,2048]{1,0:T(8,128)(2,1)S(1)} %bitcast.31, bf16[128,2048]{1,0:T(8,128)(2,1)S(1)} %bitcast.35, ...), custom_call_target="tpu_custom_call" | custom-call | tf_op jit(solution)/shard_map/pallas_call | solution.py:988
  66.4 1.9 %collective-permute-done.10.arrived_ref = bf16[2048,128]{1,0:T(8,128)(2,1)S(1)} collective-permute-done((bf16[2048,128]{1,0:T(8,128)(2,1)S(1)}, bf16[2048,128]{1,0:T(8,128)(2,1)S(1)}, u32[]{:S(2)}, u32[]{:S(2)}) %collective-permute-start.10) | collective-permute-done | bytes 524320 | tf_op jit(solution)/shard_map/ppermute | solution.py:999
  68.3 6.8 %shard_map.141 = (f32[128,2048]{1,0:T(8,128)S(1)}, f32[128,2048]{1,0:T(8,128)S(1)}, bf16[128,256]{1,0:T(8,128)(2,1)S(1)}, bf16[128,32]{1,0:T(8,128)(2,1)S(1)}, f32[2,2048]{1,0:T(2,128)S(1)}) custom-call(s32[2]{0:T(128)S(1)} %pad_add_fusion.ids_ref, bf16[2048,128]{1,0:T(8,128)(2,1)S(1)} %collective-permute-done.10.arrived_ref, ...), custom_call_target="tpu_custom_call" | custom-call | tf_op jit(solution)/shard_map/pallas_call | solution.py:1001
  75.2 1.3 %shard_map.142 = (bf16[4,152,128]{2,1,0:T(8,128)(2,1)S(1)}, bf16[4,152,128]{2,1,0:T(8,128)(2,1)S(1)}, bf16[4,152,128]{2,1,0:T(8,128)(2,1)S(1)}, bf16[4,152,128]{...) custom-call(s32[2]{0:T(128)S(1)} %pad_add_fusion.ids_ref, ...), custom_call_target="tpu_custom_call" | custom-call | tf_op jit(solution)/shard_map/pallas_call | solution.py:1019
  78.0 2.0 %collective-permute-start.13 = (bf16[4,152,128]{2,1,0:T(8,128)(2,1)S(1)}, bf16[4,152,128]{2,1,0:T(8,128)(2,1)S(1)}, u32[]{:S(2)}, u32[]{:S(2)}) collective-permute-start(bf16[4,152,128]{2,1,0:T(8,128)(2,1)S(1)} %add_convert_fusion.3), channel_id=1, source_target_pairs={{0,2},{2,0},{4,6},{6,4},{8,10},{10,8},{12,14},{14,12},{16,18},{18,... | collective-permute-start | bytes 466952 | tf_op jit(solution)/shard_map/ppermute | solution.py:895
  80.1 1.5 %collective-permute-start.15 = (bf16[4,152,128]{2,1,0:T(8,128)(2,1)S(1)}, bf16[4,152,128]{2,1,0:T(8,128)(2,1)S(1)}, u32[]{:S(2)}, u32[]{:S(2)}) collective-permute-start(bf16[4,152,128]{2,1,0:T(8,128)(2,1)S(1)} %add_convert_fusion.2), channel_id=1, source_target_pairs={{0,4},{2,6},{4,0},{6,2},{8,12},{10,14},{12,8},{14,10},{16,20},{18,... | collective-permute-start | bytes 466952 | tf_op jit(solution)/shard_map/ppermute | solution.py:895
  82.1 6.8 %all-to-all-done.1.came_ref = bf16[16,2,8,2048]{3,2,1,0:T(8,128)(2,1)S(1)} async-done(((bf16[16,2,8,2048]{3,2,1,0:T(8,128)(2,1)}), bf16[16,2,8,2048]{3,2,1,0:T(8,128)(2,1)S(1)}, u32[]{:S(2)}, u32[]{:S(2)}) %all-to-all-start.1) | async-done | bytes 1048608 | tf_op jit(solution)/shard_map/all_to_all | solution.py:44
  89.0 1.2 %copy-done.3 = f32[128,2048]{1,0:T(8,128)S(1)} copy-done((f32[128,2048]{1,0:T(8,128)S(1)}, f32[128,2048]{1,0:T(8,128)}, u32[]{:S(2)}) %copy-start.3) | copy-done | bytes 1048600
  90.2 1.2 %copy-done.5 = f32[128,2048]{1,0:T(8,128)S(1)} copy-done((f32[128,2048]{1,0:T(8,128)S(1)}, f32[128,2048]{1,0:T(8,128)}, u32[]{:S(2)}) %copy-start.5) | copy-done | bytes 1048600
  91.4 1.7 %shard_map.143 = (bf16[128,2048]{1,0:T(8,128)(2,1)}, bf16[128,2048]{1,0:T(8,128)(2,1)}) custom-call(bf16[128,2048]{1,0:T(8,128)(2,1)S(1)} %bitcast.33, f32[128,1]{1,0:T(8,128)S(1)} %get-tuple-element.60.refs_5_.inverse_ref, f32[1,2048]{1,0:T(1,128)S(1)} %get-tuple-element.50.refs_1_.refs_3_.gain_ref, f32[128,2048]{1,0:T(8,128)S(1)} %copy-done.3, ...), custom_call_target="tpu_custom_call" | custom-call | tf_op jit(solution)/shard_map/pallas_call | solution.py:1023
  93.3 3.3 %collective-permute-start.18 = (bf16[152,128]{1,0:T(8,128)(2,1)S(1)}, bf16[152,128]{1,0:T(8,128)(2,1)S(1)}, u32[]{:S(2)}, u32[]{:S(2)}) collective-permute-start(bf16[152,128]{1,0:T(8,128)(2,1)S(1)} %get-tuple-element.91), channel_id=1, source_target_pairs={{0,8},{2,10},{4,12},{6,14},{8,0},{10,2},{12,4},{14,6},{16,24},{18,... | collective-permute-start | bytes 116744 | tf_op jit(solution)/shard_map/ppermute | solution.py:895
  96.6 1.4 %collective-permute-start.20 = (bf16[152,128]{1,0:T(8,128)(2,1)S(1)}, bf16[152,128]{1,0:T(8,128)(2,1)S(1)}, u32[]{:S(2)}, u32[]{:S(2)}) collective-permute-start(bf16[152,128]{1,0:T(8,128)(2,1)S(1)} %get-tuple-element.92), channel_id=1, source_target_pairs={{0,24},{2,26},{4,28},{6,30},{8,16},{10,18},{12,20},{14,22},{16,8},... | collective-permute-start | bytes 116744 | tf_op jit(solution)/shard_map/ppermute | solution.py:895
  98.5 3.8 %collective-permute-done.20 = bf16[152,128]{1,0:T(8,128)(2,1)S(1)} collective-permute-done((bf16[152,128]{1,0:T(8,128)(2,1)S(1)}, bf16[152,128]{1,0:T(8,128)(2,1)S(1)}, u32[]{:S(2)}, u32[]{:S(2)}) %collective-permute-start.20) | collective-permute-done | bytes 38944 | tf_op jit(solution)/shard_map/ppermute | solution.py:895
  104.5 1.2 %shard_map.145 = (f32[128,256]{1,0:T(8,128)}, f32[32,128]{1,0:T(8,128)}) custom-call(s32[2]{0:T(128)S(1)} %pad_add_fusion.ids_ref, f32[152,128]{1,0:T(8,128)S(1)} %fusion.1.sums_ref.own_ref, f32[152,128]{1,0:T(8,128)S(1)} %collective-permute-done.21.other_ref), custom_call_target="tpu_custom_call" | custom-call | tf_op jit(solution)/shard_map/pallas_call | solution.py:1034
  (68 shorter events, 9.6 us)
Async XLA Ops:
  4.4 49.1 %all-to-all-start = ((bf16[16,2,8,2048]{3,2,1,0:T(8,128)(2,1)}), bf16[16,2,8,2048]{3,2,1,0:T(8,128)(2,1)S(1)}, u32[]{:S(2)}, u32[]{:S(2)}) async-start(bf16[16,2,8,2048]{3,2,1,0:T(8,128)(2,1)} %get-tuple-element.51), calls=%async_computation | async-start | bytes 2097152 | tf_op jit(solution)/shard_map/all_to_all | solution.py:44
  12.7 22.8 %collective-permute-start.2 = (bf16[152,128]{1,0:T(8,128)(2,1)S(1)}, bf16[152,128]{1,0:T(8,128)(2,1)S(1)}, u32[]{:S(2)}, u32[]{:S(2)}) collective-permute-start(bf16[152,128]{1,0:T(8,128)(2,1)S(1)} %get-tuple-element.48), channel_id=1, source_target_pairs={{0,24},{2,26},{4,28},{6,30},{8,16},{10,18},{12,20},{14,22},{16,8},... | collective-permute-start | bytes 116744 | tf_op jit(solution)/shard_map/ppermute | solution.py:877
  16.4 25.3 %collective-permute-start.1 = (bf16[152,128]{1,0:T(8,128)(2,1)S(1)}, bf16[152,128]{1,0:T(8,128)(2,1)S(1)}, u32[]{:S(2)}, u32[]{:S(2)}) collective-permute-start(bf16[152,128]{1,0:T(8,128)(2,1)S(1)} %get-tuple-element.48), channel_id=1, source_target_pairs={{0,16},{2,18},{4,20},{6,22},{8,24},{10,26},{12,28},{14,30},{16,0},... | collective-permute-start | bytes 116744 | tf_op jit(solution)/shard_map/ppermute | solution.py:877
  16.4 25.3 %collective-permute-start = (bf16[152,128]{1,0:T(8,128)(2,1)S(1)}, bf16[152,128]{1,0:T(8,128)(2,1)S(1)}, u32[]{:S(2)}, u32[]{:S(2)}) collective-permute-start(bf16[152,128]{1,0:T(8,128)(2,1)S(1)} %get-tuple-element.48), channel_id=1, source_target_pairs={{0,8},{2,10},{4,12},{6,14},{8,0},{10,2},{12,4},{14,6},{16,24},{18,... | collective-permute-start | bytes 116744 | tf_op jit(solution)/shard_map/ppermute | solution.py:877
  41.8 7.5 %collective-permute-start.5 = (bf16[4,152,128]{2,1,0:T(8,128)(2,1)S(1)}, bf16[4,152,128]{2,1,0:T(8,128)(2,1)S(1)}, u32[]{:S(2)}, u32[]{:S(2)}) collective-permute-start(bf16[4,152,128]{2,1,0:T(8,128)(2,1)S(1)} %pad_maximum_fusion.refs_0_), channel_id=1, source_target_pairs={{0,6},{2,4},{4,2},{6,0},{8,14},{10,12},{12,10},{14,8},{16,22},{18,... | collective-permute-start | bytes 466952 | tf_op jit(solution)/shard_map/ppermute | solution.py:877
  44.3 6.5 %collective-permute-start.4 = (bf16[4,152,128]{2,1,0:T(8,128)(2,1)S(1)}, bf16[4,152,128]{2,1,0:T(8,128)(2,1)S(1)}, u32[]{:S(2)}, u32[]{:S(2)}) collective-permute-start(bf16[4,152,128]{2,1,0:T(8,128)(2,1)S(1)} %pad_maximum_fusion.refs_0_), channel_id=1, source_target_pairs={{0,4},{2,6},{4,0},{6,2},{8,12},{10,14},{12,8},{14,10},{16,20},{18,... | collective-permute-start | bytes 466952 | tf_op jit(solution)/shard_map/ppermute | solution.py:877
  44.7 6.2 %collective-permute-start.3 = (bf16[4,152,128]{2,1,0:T(8,128)(2,1)S(1)}, bf16[4,152,128]{2,1,0:T(8,128)(2,1)S(1)}, u32[]{:S(2)}, u32[]{:S(2)}) collective-permute-start(bf16[4,152,128]{2,1,0:T(8,128)(2,1)S(1)} %pad_maximum_fusion.refs_0_), channel_id=1, source_target_pairs={{0,2},{2,0},{4,6},{6,4},{8,10},{10,8},{12,14},{14,12},{16,18},{18,... | collective-permute-start | bytes 466952 | tf_op jit(solution)/shard_map/ppermute | solution.py:877
  45.3 6.7 %collective-permute-start.6 = (bf16[4,152,128]{2,1,0:T(8,128)(2,1)S(1)}, bf16[4,152,128]{2,1,0:T(8,128)(2,1)S(1)}, u32[]{:S(2)}, u32[]{:S(2)}) collective-permute-start(bf16[4,152,128]{2,1,0:T(8,128)(2,1)S(1)} %pad_maximum_fusion.refs_0_), channel_id=1, source_target_pairs={{0,1},{1,0},{2,3},{3,2},{4,5},{5,4},{6,7},{7,6},{8,9},{9,8},{10,11... | collective-permute-start | bytes 466952 | tf_op jit(solution)/shard_map/ppermute | solution.py:958
  49.3 2.8 %collective-permute-start.9 = (bf16[4,152,128]{2,1,0:T(8,128)(2,1)S(1)}, bf16[4,152,128]{2,1,0:T(8,128)(2,1)S(1)}, u32[]{:S(2)}, u32[]{:S(2)}) collective-permute-start(bf16[4,152,128]{2,1,0:T(8,128)(2,1)S(1)} %collective-permute-done.5.refs_3_), channel_id=1, source_target_pairs={{0,1},{1,0},{2,3},{3,2},{4,5},{5,4},{6,7},{7,6},{8,9},{9,8},{10,11... | collective-permute-start | bytes 466952 | tf_op jit(solution)/shard_map/ppermute | solution.py:958
  50.8 1.4 %collective-permute-start.8 = (bf16[4,152,128]{2,1,0:T(8,128)(2,1)S(1)}, bf16[4,152,128]{2,1,0:T(8,128)(2,1)S(1)}, u32[]{:S(2)}, u32[]{:S(2)}) collective-permute-start(bf16[4,152,128]{2,1,0:T(8,128)(2,1)S(1)} %collective-permute-done.4.refs_2_), channel_id=1, source_target_pairs={{0,1},{1,0},{2,3},{3,2},{4,5},{5,4},{6,7},{7,6},{8,9},{9,8},{10,11... | collective-permute-start | bytes 466952 | tf_op jit(solution)/shard_map/ppermute | solution.py:958
  50.9 1.5 %collective-permute-start.7 = (bf16[4,152,128]{2,1,0:T(8,128)(2,1)S(1)}, bf16[4,152,128]{2,1,0:T(8,128)(2,1)S(1)}, u32[]{:S(2)}, u32[]{:S(2)}) collective-permute-start(bf16[4,152,128]{2,1,0:T(8,128)(2,1)S(1)} %collective-permute-done.3.refs_1_), channel_id=1, source_target_pairs={{0,1},{1,0},{2,3},{3,2},{4,5},{5,4},{6,7},{7,6},{8,9},{9,8},{10,11... | collective-permute-start | bytes 466952 | tf_op jit(solution)/shard_map/ppermute | solution.py:958
  59.9 29.1 %all-to-all-start.1 = ((bf16[16,2,8,2048]{3,2,1,0:T(8,128)(2,1)}), bf16[16,2,8,2048]{3,2,1,0:T(8,128)(2,1)S(1)}, u32[]{:S(2)}, u32[]{:S(2)}) async-start(bf16[16,2,8,2048]{3,2,1,0:T(8,128)(2,1)} %get-tuple-element.78), calls=%async_computation.1 | async-start | bytes 2097152 | tf_op jit(solution)/shard_map/all_to_all | solution.py:44
  66.4 2.0 %collective-permute-start.10 = (bf16[2048,128]{1,0:T(8,128)(2,1)S(1)}, bf16[2048,128]{1,0:T(8,128)(2,1)S(1)}, u32[]{:S(2)}, u32[]{:S(2)}) collective-permute-start(bf16[2048,128]{1,0:T(8,128)(2,1)S(1)} %get-tuple-element.57), channel_id=1, source_target_pairs={{0,1},{1,0},{2,3},{3,2},{4,5},{5,4},{6,7},{7,6},{8,9},{9,8},{10,11... | collective-permute-start | bytes 1572872 | tf_op jit(solution)/shard_map/ppermute | solution.py:999
  76.5 1.4 %collective-permute-start.12 = (bf16[4,152,128]{2,1,0:T(8,128)(2,1)S(1)}, bf16[4,152,128]{2,1,0:T(8,128)(2,1)S(1)}, u32[]{:S(2)}, u32[]{:S(2)}) collective-permute-start(bf16[4,152,128]{2,1,0:T(8,128)(2,1)S(1)} %get-tuple-element.71), channel_id=1, source_target_pairs={{0,1},{1,0},{2,3},{3,2},{4,5},{5,4},{6,7},{7,6},{8,9},{9,8},{10,11... | collective-permute-start | bytes 466952 | tf_op jit(solution)/shard_map/ppermute | solution.py:1022
  76.7 5.4 %collective-permute-start.11 = (bf16[4,152,128]{2,1,0:T(8,128)(2,1)S(1)}, bf16[4,152,128]{2,1,0:T(8,128)(2,1)S(1)}, u32[]{:S(2)}, u32[]{:S(2)}) collective-permute-start(bf16[4,152,128]{2,1,0:T(8,128)(2,1)S(1)} %get-tuple-element.69), channel_id=1, source_target_pairs={{0,1},{1,0},{2,3},{3,2},{4,5},{5,4},{6,7},{7,6},{8,9},{9,8},{10,11... | collective-permute-start | bytes 466952 | tf_op jit(solution)/shard_map/ppermute | solution.py:1022
  77.1 2.9 %collective-permute-start.14 = (bf16[4,152,128]{2,1,0:T(8,128)(2,1)S(1)}, bf16[4,152,128]{2,1,0:T(8,128)(2,1)S(1)}, u32[]{:S(2)}, u32[]{:S(2)}) collective-permute-start(bf16[4,152,128]{2,1,0:T(8,128)(2,1)S(1)} %get-tuple-element.73), channel_id=1, source_target_pairs={{0,1},{1,0},{2,3},{3,2},{4,5},{5,4},{6,7},{7,6},{8,9},{9,8},{10,11... | collective-permute-start | bytes 466952 | tf_op jit(solution)/shard_map/ppermute | solution.py:1022
  77.2 4.4 %collective-permute-start.16 = (bf16[4,152,128]{2,1,0:T(8,128)(2,1)S(1)}, bf16[4,152,128]{2,1,0:T(8,128)(2,1)S(1)}, u32[]{:S(2)}, u32[]{:S(2)}) collective-permute-start(bf16[4,152,128]{2,1,0:T(8,128)(2,1)S(1)} %get-tuple-element.75), channel_id=1, source_target_pairs={{0,1},{1,0},{2,3},{3,2},{4,5},{5,4},{6,7},{7,6},{8,9},{9,8},{10,11... | collective-permute-start | bytes 466952 | tf_op jit(solution)/shard_map/ppermute | solution.py:1022
  78.0 15.1 %collective-permute-start.13 = (bf16[4,152,128]{2,1,0:T(8,128)(2,1)S(1)}, bf16[4,152,128]{2,1,0:T(8,128)(2,1)S(1)}, u32[]{:S(2)}, u32[]{:S(2)}) collective-permute-start(bf16[4,152,128]{2,1,0:T(8,128)(2,1)S(1)} %add_convert_fusion.3), channel_id=1, source_target_pairs={{0,2},{2,0},{4,6},{6,4},{8,10},{10,8},{12,14},{14,12},{16,18},{18,... | collective-permute-start | bytes 466952 | tf_op jit(solution)/shard_map/ppermute | solution.py:895
  80.1 13.1 %collective-permute-start.15 = (bf16[4,152,128]{2,1,0:T(8,128)(2,1)S(1)}, bf16[4,152,128]{2,1,0:T(8,128)(2,1)S(1)}, u32[]{:S(2)}, u32[]{:S(2)}) collective-permute-start(bf16[4,152,128]{2,1,0:T(8,128)(2,1)S(1)} %add_convert_fusion.2), channel_id=1, source_target_pairs={{0,4},{2,6},{4,0},{6,2},{8,12},{10,14},{12,8},{14,10},{16,20},{18,... | collective-permute-start | bytes 466952 | tf_op jit(solution)/shard_map/ppermute | solution.py:895
  81.6 11.5 %collective-permute-start.17 = (bf16[4,152,128]{2,1,0:T(8,128)(2,1)S(1)}, bf16[4,152,128]{2,1,0:T(8,128)(2,1)S(1)}, u32[]{:S(2)}, u32[]{:S(2)}) collective-permute-start(bf16[4,152,128]{2,1,0:T(8,128)(2,1)S(1)} %add_convert_fusion.1), channel_id=1, source_target_pairs={{0,6},{2,4},{4,2},{6,0},{8,14},{10,12},{12,10},{14,8},{16,22},{18,... | collective-permute-start | bytes 466952 | tf_op jit(solution)/shard_map/ppermute | solution.py:895
  93.3 5.3 %collective-permute-start.18 = (bf16[152,128]{1,0:T(8,128)(2,1)S(1)}, bf16[152,128]{1,0:T(8,128)(2,1)S(1)}, u32[]{:S(2)}, u32[]{:S(2)}) collective-permute-start(bf16[152,128]{1,0:T(8,128)(2,1)S(1)} %get-tuple-element.91), channel_id=1, source_target_pairs={{0,8},{2,10},{4,12},{6,14},{8,0},{10,2},{12,4},{14,6},{16,24},{18,... | collective-permute-start | bytes 116744 | tf_op jit(solution)/shard_map/ppermute | solution.py:895
  96.6 5.8 %collective-permute-start.20 = (bf16[152,128]{1,0:T(8,128)(2,1)S(1)}, bf16[152,128]{1,0:T(8,128)(2,1)S(1)}, u32[]{:S(2)}, u32[]{:S(2)}) collective-permute-start(bf16[152,128]{1,0:T(8,128)(2,1)S(1)} %get-tuple-element.92), channel_id=1, source_target_pairs={{0,24},{2,26},{4,28},{6,30},{8,16},{10,18},{12,20},{14,22},{16,8},... | collective-permute-start | bytes 116744 | tf_op jit(solution)/shard_map/ppermute | solution.py:895
  98.0 5.2 %collective-permute-start.19 = (bf16[152,128]{1,0:T(8,128)(2,1)S(1)}, bf16[152,128]{1,0:T(8,128)(2,1)S(1)}, u32[]{:S(2)}, u32[]{:S(2)}) collective-permute-start(bf16[152,128]{1,0:T(8,128)(2,1)S(1)} %get-tuple-element.93), channel_id=1, source_target_pairs={{0,16},{2,18},{4,20},{6,22},{8,24},{10,26},{12,28},{14,30},{16,0},... | collective-permute-start | bytes 116744 | tf_op jit(solution)/shard_map/ppermute | solution.py:895
  103.2 1.3 %collective-permute-start.21 = (f32[152,128]{1,0:T(8,128)S(1)}, f32[152,128]{1,0:T(8,128)S(1)}, u32[]{:S(2)}, u32[]{:S(2)}) collective-permute-start(f32[152,128]{1,0:T(8,128)S(1)} %fusion.1.sums_ref.own_ref), channel_id=1, source_target_pairs={{0,1},{1,0},{2,3},{3,2},{4,5},{5,4},{6,7},{7,6},{8,9},{9,8},{10,11... | collective-permute-start | bytes 233480 | tf_op jit(solution)/shard_map/ppermute | solution.py:1027
  (12 other events, 46.4 us)
